TPU v7x, 32 devices: a whole 2x2x4 slice. The times are simulated.
32 devices in a mesh: ctx: 8 (over z, x), head: 4 (over y, core).
Axes of the slice: x: 2, y: 2, z: 4, core: 2. Of those that a mesh axis runs over, the one named last changes fastest.
Arguments:
- query: bfloat16 [16384, 8192], P(('ctx', 'head')), as said below
- key: bfloat16 [16384, 1024], P(('ctx', 'head')), as said below
- value: bfloat16 [16384, 1024], P(('ctx', 'head')), may hold values from -6 to 6
- doc_ids: int32 [128], replicated, may hold values from 0 to 20, never falling along the last dimension, each value on 1 to 8 neighbouring positions
- plan: int32 [128], replicated, may hold values from 0 to 127, as said below
Outputs:
- attended: bfloat16 [16384, 8192], P('ctx', 'head')
Inputs may be any that keep to these rules, and one draw needn't show every extreme that they name: `doc_ids`: block ids never fall; each document holds 1 to 8 blocks, one exactly 8. `plan`: A permutation of the 128 blocks. Output positions k * 16 to (k + 1) * 16 - 1 belong to context shard k. Every shard receives 16 blocks; of the blocks j * 16 to (j + 1) * 16 - 1 at most 2 go to one shard, and exactly 2 to some shard. `query`: real values; no structure promised. `key`: real values; no structure promised.
All inputs are finite; a program needn't handle non-finite values.
Results may differ from a plain program's by a relative error of at most 0.0038.
Values may be sent and summed in bfloat16 or wider, within the bound.
A program may use at most 128 MiB of HBM per device.

v0:
```python
import functools
import math

import jax
import jax.numpy as jnp
from jax import lax
from jax.experimental import pallas as pl
from jax.experimental.pallas import tpu as pltpu
from jax.sharding import PartitionSpec as P


HD = 128
BLK = 128
MAXDOC = 8
ROW_HEADS = 2


def attend_kernel(heads, block_ref, count_ref, q_ref, kv_ref, o_ref):
    factor = math.log2(math.e) / math.sqrt(HD)
    rows = ROW_HEADS * BLK
    row_pos = lax.rem(lax.broadcasted_iota(jnp.int32, (rows, BLK), 0), BLK)
    causal = lax.broadcasted_iota(jnp.int32, (rows, BLK), 1) <= row_pos

    def body(pairs, slot, block, count):
        width = 2 * pairs * BLK
        first = pl.multiple_of((block + MAXDOC - 2 * pairs) * BLK, BLK)
        q_rows = pl.ds(pl.multiple_of(block * BLK, BLK), BLK)
        keys = kv_ref[pl.ds(first, width), :HD]
        values = kv_ref[pl.ds(first, width), HD:]
        inside = jnp.full((rows, BLK), count - (2 * pairs - 1), jnp.int32) > 0
        for step in range(heads // ROW_HEADS):
            base = step * ROW_HEADS * HD
            queries = jnp.concatenate(
                [q_ref[q_rows, base + i * HD : base + (i + 1) * HD] for i in range(ROW_HEADS)],
                axis=0,
            )
            scores = lax.dot_general(
                queries, keys, (((1,), (1,)), ((), ())), preferred_element_type=jnp.float32
            )
            parts = [scores[:, i * BLK : (i + 1) * BLK] for i in range(2 * pairs)]
            parts[0] = jnp.where(inside, parts[0], -jnp.inf)
            parts[-1] = jnp.where(causal, parts[-1], -jnp.inf)
            top = functools.reduce(jnp.maximum, parts)
            top = jnp.max(top, axis=1, keepdims=True)
            parts = [jnp.exp2((part - top) * factor) for part in parts]
            total = jnp.sum(functools.reduce(jnp.add, parts), axis=1, keepdims=True)
            weights = jnp.concatenate([part.astype(jnp.bfloat16) for part in parts], axis=1)
            mixed = jnp.dot(weights, values, preferred_element_type=jnp.float32) / total
            mixed = mixed.astype(o_ref.dtype)
            for i in range(ROW_HEADS):
                o_ref[slot, :, base + i * HD : base + (i + 1) * HD] = mixed[
                    i * BLK : (i + 1) * BLK
                ]

    def one(slot, carry):
        block = block_ref[slot]
        count = count_ref[slot]
        for pairs in range(1, MAXDOC // 2 + 1):

            @pl.when((count + 1) // 2 == pairs)
            def _():
                body(pairs, slot, block, count)

        return carry

    lax.fori_loop(0, o_ref.shape[0], one, 0)


def attend(slot_block, slot_count, queries, window):
    slots = slot_block.shape[0]
    width = queries.shape[1]
    heads = width // HD
    flops = 4 * slots * heads * BLK * BLK * HD * 5
    return pl.pallas_call(
        functools.partial(attend_kernel, heads),
        out_shape=jax.ShapeDtypeStruct((slots, BLK, width), jnp.bfloat16),
        in_specs=[pl.BlockSpec(memory_space=pltpu.SMEM)] * 2
        + [pl.BlockSpec(memory_space=pltpu.VMEM)] * 2,
        out_specs=pl.BlockSpec(memory_space=pltpu.VMEM),
        cost_estimate=pl.CostEstimate(
            flops=flops, transcendentals=0, bytes_accessed=4 * queries.size + 2 * window.size
        ),
        name="attend",
    )(slot_block, slot_count, queries, window)


def place_kernel(first, slot_ref, x_ref, *rest):
    o_ref, sems = rest[-2:]
    blocks = o_ref.shape[0] // BLK
    width = x_ref.shape[2]

    def copy(i):
        return pltpu.make_async_copy(
            x_ref.at[slot_ref[i]],
            o_ref.at[pl.ds(i * BLK, BLK), pl.ds(first, width)],
            sems.at[i],
        )

    for i in range(blocks):
        copy(i).start()
    for i in range(blocks):
        copy(i).wait()


def place(slot_of, received, so_far, first, full):
    blocks = slot_of.shape[0]
    width = received.shape[2]
    in_specs = [pl.BlockSpec(memory_space=pltpu.SMEM), pl.BlockSpec(memory_space=pltpu.VMEM)]
    operands = [slot_of, received]
    aliases = {}
    if so_far is not None:
        in_specs.append(pl.BlockSpec(memory_space=pl.ANY))
        operands.append(so_far)
        aliases = {2: 0}
    return pl.pallas_call(
        functools.partial(place_kernel, first),
        out_shape=jax.ShapeDtypeStruct((blocks * BLK, full), jnp.bfloat16),
        in_specs=in_specs,
        out_specs=pl.BlockSpec(memory_space=pl.ANY),
        scratch_shapes=[pltpu.SemaphoreType.DMA((blocks,))],
        cost_estimate=pl.CostEstimate(
            flops=0, transcendentals=0, bytes_accessed=4 * blocks * BLK * width
        ),
        input_output_aliases=aliases,
        name="place",
    )(*operands)


def shifted(shard, axis, by):
    count = lax.axis_size(axis)
    pairs = [(i, i + by) for i in range(count) if 0 <= i + by < count]
    return lax.ppermute(shard, axis, pairs)


def shards(query, key, value, doc_ids, plan):
    head_count = lax.axis_size("head")
    shard_count = lax.axis_size("ctx")
    local_rows = query.shape[0]
    rows = head_count * local_rows
    blocks_here = rows // BLK
    q_width = query.shape[1] // head_count
    kv_width = key.shape[1] // head_count
    kv_heads = kv_width // HD
    group = q_width // HD // kv_heads
    head = lax.axis_index("head")

    def pieces(kv_head, first, heads, with_kv, of_head):
        wanted = [(query, of_head * q_width + first * HD, heads * HD)]
        if with_kv:
            start = of_head * kv_width + kv_head * HD
            wanted += [(key, start, HD), (value, start, HD)]
        return wanted

    def all_pairs(wanted_of):
        parts = jnp.stack(
            [
                jnp.concatenate([x[:, s : s + w] for x, s, w in wanted_of(h)], axis=1)
                for h in range(head_count)
            ]
        )
        parts = lax.all_to_all(parts, "head", split_axis=0, concat_axis=0, tiled=True)
        return parts.reshape(rows, parts.shape[2])

    def by_permutes(wanted_of):
        def part(of_head):
            return jnp.concatenate(
                [
                    lax.dynamic_slice(x, (0, s), (local_rows, w))
                    for x, s, w in wanted_of(of_head)
                ],
                axis=1,
            )

        whole = None
        for step in range(head_count):
            other = jnp.bitwise_xor(head, step)
            piece = part(other)
            if step:
                piece = lax.ppermute(
                    piece, "head", [(h, h ^ step) for h in range(head_count)]
                )
            if whole is None:
                whole = jnp.zeros((rows, piece.shape[1]), piece.dtype)
            whole = lax.dynamic_update_slice(whole, piece, (other * local_rows, 0))
        return whole

    def windowed(kv):
        before = shifted(kv[rows - (MAXDOC - 1) * BLK :], "ctx", 1)
        return jnp.concatenate([before, kv], axis=0)

    shard = lax.axis_index("ctx")
    doc_start = jnp.sum((doc_ids[None, :] < doc_ids[:, None]).astype(jnp.int32), axis=1)
    counts = jnp.arange(doc_ids.shape[0], dtype=jnp.int32) - doc_start + 1
    own_counts = lax.dynamic_slice_in_dim(counts, shard * blocks_here, blocks_here)
    capacity = -(-blocks_here // shard_count)
    slots = shard_count * capacity
    grid = plan.reshape(shard_count, blocks_here)
    source = grid // blocks_here
    local = grid % blocks_here
    iota = jnp.arange(blocks_here, dtype=jnp.int32)
    lower = (iota[None, :] < iota[:, None])[None]
    rank = jnp.sum(
        ((source[:, :, None] == source[:, None, :]) & lower).astype(jnp.int32), axis=2
    )
    hit = (source == shard)[:, None, :] & (
        rank[:, None, :] == jnp.arange(capacity, dtype=jnp.int32)[None, :, None]
    )
    hit = hit.reshape(slots, blocks_here)
    local = jnp.broadcast_to(local[:, None, :], (shard_count, capacity, blocks_here))
    local = local.reshape(slots, blocks_here)
    slot_block = jnp.sum(jnp.where(hit, local, 0), axis=1)
    one_hot = hit[:, :, None] & (local[:, :, None] == iota[None, None, :])
    slot_count = jnp.sum(jnp.where(one_hot, own_counts[None, None, :], 0), axis=(1, 2))
    mine = lax.dynamic_index_in_dim(source * capacity + rank, shard, 0, False)

    chunks = []
    for kv_head in range(kv_heads):
        sizes = [group // 4, group // 4, group // 2] if kv_head == 0 else [group // 2] * 2
        start = kv_head * group
        for i, size in enumerate(sizes):
            chunks.append((kv_head, start, size, i == 0))
            start += size

    result = None
    window = None
    arrived = []
    for at, (kv_head, first, heads, fresh) in enumerate(chunks):
        if at == 0:
            kv = all_pairs(
                lambda h: [(x, h * kv_width, HD) for x in (key, value)]
            )
            q = all_pairs(lambda h: [(query, h * q_width, heads * HD)])
        else:
            both = by_permutes(functools.partial(pieces, kv_head, first, heads, fresh))
            q = both[:, : heads * HD]
            kv = both[:, heads * HD :]
        arrived.append((kv_head, first, heads, q, windowed(kv) if fresh else None))
    for kv_head, first, heads, q, fresh_window in arrived:
        window = window if fresh_window is None else fresh_window
        out = attend(slot_block, slot_count, q, window)
        received = lax.all_to_all(out, "ctx", split_axis=0, concat_axis=0, tiled=True)
        result = place(mine, received, result, first * HD, q_width)
    return result


def solution(mesh):
    return jax.shard_map(
        shards,
        mesh=mesh,
        in_specs=(
            P(("ctx", "head"), None),
            P(("ctx", "head"), None),
            P(("ctx", "head"), None),
            P(),
            P(),
        ),
        out_specs=P("ctx", "head"),
        check_vma=False,
    )
```

profile of v0, /device:TPU:0, one launch (start us, length us, event | category | flops | bytes accessed | tf_op | source)
XLA Modules:
  0.0 339.8 jit_solution(8202639438324033712)
XLA Ops:
  0.0 2.6 fusion.5
  3.9 4.3 %all-to-all-start.2 = ((bf16[4,512,256]{2,1,0:T(8,128)(2,1)}), bf16[4,512,256]{2,1,0:T(8,128)(2,1)S(1)}, u32[]{:S(2)}, u32[]{:S(2)}) async-start(bf16[4,512,256]{2,1,0:T(8,128)(2,1)} %pad_maximum_fusion.2), calls=%async_computation.2 | async-start | bytes 2097152 | tf_op jit(solution)/shard_map/all_to_all | solution.py:161
  13.3 9.3 %all-to-all-done.2 = bf16[4,512,256]{2,1,0:T(8,128)(2,1)S(1)} async-done(((bf16[4,512,256]{2,1,0:T(8,128)(2,1)}), bf16[4,512,256]{2,1,0:T(8,128)(2,1)S(1)}, u32[]{:S(2)}, u32[]{:S(2)}) %all-to-all-start.2) | async-done | bytes 1048608 | tf_op jit(solution)/shard_map/all_to_all | solution.py:161
  22.6 3.5 %all-to-all-start.5 = ((bf16[4,512,256]{2,1,0:T(8,128)(2,1)}), bf16[4,512,256]{2,1,0:T(8,128)(2,1)S(1)}, u32[]{:S(2)}, u32[]{:S(2)}) async-start(bf16[4,512,256]{2,1,0:T(8,128)(2,1)} %pad_maximum_fusion.3), calls=%async_computation.5 | async-start | bytes 2097152 | tf_op jit(solution)/shard_map/all_to_all | solution.py:161
  26.9 4.9 %collective-permute-start.10 = (bf16[896,256]{1,0:T(8,128)(2,1)}, bf16[896,256]{1,0:T(8,128)(2,1)}, u32[]{:S(2)}, u32[]{:S(2)}) collective-permute-start(bf16[896,256]{1,0:T(8,128)(2,1)} %slice.68), channel_id=1, source_target_pairs={{0,4},{4,8},{8,12},{12,16},{16,20},{20,24},{24,28},{1,5},{5,9},{9,... | collective-permute-start | bytes 1376264 | tf_op jit(solution)/shard_map/ppermute | solution.py:132
  38.0 3.6 %collective-permute-done.10 = bf16[896,256]{1,0:T(8,128)(2,1)} collective-permute-done((bf16[896,256]{1,0:T(8,128)(2,1)}, bf16[896,256]{1,0:T(8,128)(2,1)}, u32[]{:S(2)}, u32[]{:S(2)}) %collective-permute-start.10) | collective-permute-done | bytes 458784 | tf_op jit(solution)/shard_map/ppermute | solution.py:132
  44.9 11.1 %attend.9 = bf16[16,128,256]{2,1,0:T(8,128)(2,1)} custom-call(s32[16]{0:T(128)} %reduce_sum.40.block_ref, s32[16]{0:T(128)} %select_reduce_fusion.count_ref, bf16[2048,256]{1,0:T(8,128)(2,1)} %bitcast.24, bf16[2944,256]{1,0:T(8,128)(2,1)} %pad_maximum_fusion.1.kv_ref), custom_call_target="tpu_custom_call" | custom-call | flops 1342177280 | bytes 3604480 | tf_op jit(solution)/shard_map/attend/pallas_call | solution.py:74
  56.0 7.2 %all-to-all-start.6 = ((bf16[16,128,256]{2,1,0:T(8,128)(2,1)}), bf16[16,128,256]{2,1,0:T(8,128)(2,1)S(1)}, u32[]{:S(2)}, u32[]{:S(2)}) async-start(bf16[16,128,256]{2,1,0:T(8,128)(2,1)} %attend.9), calls=%async_computation.6 | async-start | bytes 2097152 | tf_op jit(solution)/shard_map/all_to_all | solution.py:241
  66.2 6.5 %collective-permute-done.12 = bf16[512,256]{1,0:T(8,128)(2,1)} collective-permute-done((bf16[512,256]{1,0:T(8,128)(2,1)S(1)}, bf16[512,256]{1,0:T(8,128)(2,1)}, u32[]{:S(2)}, u32[]{:S(2)}) %collective-permute-start.12) | collective-permute-done | bytes 262176 | tf_op jit(solution)/shard_map/ppermute | solution.py:179
  73.7 3.4 %collective-permute-done.13 = bf16[512,256]{1,0:T(8,128)(2,1)S(1)} collective-permute-done((bf16[512,256]{1,0:T(8,128)(2,1)S(1)}, bf16[512,256]{1,0:T(8,128)(2,1)S(1)}, u32[]{:S(2)}, u32[]{:S(2)}) %collective-permute-start.13) | collective-permute-done | bytes 262176 | tf_op jit(solution)/shard_map/ppermute | solution.py:179
  78.1 11.1 %attend.8 = bf16[16,128,256]{2,1,0:T(8,128)(2,1)} custom-call(s32[16]{0:T(128)} %reduce_sum.40.block_ref, s32[16]{0:T(128)} %select_reduce_fusion.count_ref, bf16[2048,256]{1,0:T(8,128)(2,1)} %copy-done.10, bf16[2944,256]{1,0:T(8,128)(2,1)} %pad_maximum_fusion.1.kv_ref), custom_call_target="tpu_custom_call" | custom-call | flops 1342177280 | bytes 3604480 | tf_op jit(solution)/shard_map/attend/pallas_call | solution.py:74
  89.2 6.2 %all-to-all-start.4 = ((bf16[16,128,256]{2,1,0:T(8,128)(2,1)}), bf16[16,128,256]{2,1,0:T(8,128)(2,1)S(1)}, u32[]{:S(2)}, u32[]{:S(2)}) async-start(bf16[16,128,256]{2,1,0:T(8,128)(2,1)} %attend.8), calls=%async_computation.4 | async-start | bytes 2097152 | tf_op jit(solution)/shard_map/all_to_all | solution.py:241
  96.9 4.7 %constant_dynamic-slice_fusion.2 = (bf16[512,512]{1,0:T(8,128)(2,1)S(1)}, bf16[512,512]{1,0:T(8,128)(2,1)S(1)}, bf16[512,512]{1,0:T(8,128)(2,1)S(1)}, bf16[2048,...) fusion(bf16[512,8192]{1,0:T(8,128)(2,1)} %param.5, ...), kind=kLoop, calls=%fused_computation.29 | loop fusion | bytes 11534384 | tf_op jit(solution)/shard_map/dynamic_slice | solution.py:168
  104.3 12.1 %collective-permute-done.8 = bf16[512,512]{1,0:T(8,128)(2,1)S(1)} collective-permute-done((bf16[512,512]{1,0:T(8,128)(2,1)S(1)}, bf16[512,512]{1,0:T(8,128)(2,1)S(1)}, u32[]{:S(2)}, u32[]{:S(2)}) %collective-permute-start.8) | collective-permute-done | bytes 524320 | tf_op jit(solution)/shard_map/ppermute | solution.py:179
  117.3 9.3 %collective-permute-done.9 = bf16[512,512]{1,0:T(8,128)(2,1)S(1)} collective-permute-done((bf16[512,512]{1,0:T(8,128)(2,1)S(1)}, bf16[512,512]{1,0:T(8,128)(2,1)S(1)}, u32[]{:S(2)}, u32[]{:S(2)}) %collective-permute-start.9) | collective-permute-done | bytes 524320 | tf_op jit(solution)/shard_map/ppermute | solution.py:179
  127.5 17.0 %attend.7 = bf16[16,128,512]{2,1,0:T(8,128)(2,1)} custom-call(s32[16]{0:T(128)} %reduce_sum.40.block_ref, s32[16]{0:T(128)} %select_reduce_fusion.count_ref, bf16[2048,512]{1,0:T(8,128)(2,1)} %constant_dynamic-update-slice_fusion.1.q_ref, bf16[2944,256]{1,0:T(8,128)(2,1)} %pad_maximum_fusion.1.kv_ref), custom_call_target="tpu_custom_call" | custom-call | flops 2684354560 | bytes 5701632 | tf_op jit(solution)/shard_map/attend/pallas_call | solution.py:74
  145.5 6.5 %all-to-all-start.3 = ((bf16[16,128,512]{2,1,0:T(8,128)(2,1)}), bf16[16,128,512]{2,1,0:T(8,128)(2,1)S(1)}, u32[]{:S(2)}, u32[]{:S(2)}) async-start(bf16[16,128,512]{2,1,0:T(8,128)(2,1)} %attend.7), calls=%async_computation.3 | async-start | bytes 4194304 | tf_op jit(solution)/shard_map/all_to_all | solution.py:241
  157.2 17.6 %collective-permute-done.4 = bf16[512,768]{1,0:T(8,128)(2,1)S(1)} collective-permute-done((bf16[512,768]{1,0:T(8,128)(2,1)S(1)}, bf16[512,768]{1,0:T(8,128)(2,1)S(1)}, u32[]{:S(2)}, u32[]{:S(2)}) %collective-permute-start.4) | collective-permute-done | bytes 786464 | tf_op jit(solution)/shard_map/ppermute | solution.py:179
  174.8 15.7 %collective-permute-done.5 = bf16[512,768]{1,0:T(8,128)(2,1)S(1)} collective-permute-done((bf16[512,768]{1,0:T(8,128)(2,1)S(1)}, bf16[512,768]{1,0:T(8,128)(2,1)S(1)}, u32[]{:S(2)}, u32[]{:S(2)}) %collective-permute-start.5) | collective-permute-done | bytes 786464 | tf_op jit(solution)/shard_map/ppermute | solution.py:179
  190.7 4.2 %collective-permute-start.6 = (bf16[896,256]{1,0:T(8,128)(2,1)S(1)}, bf16[896,256]{1,0:T(8,128)(2,1)S(1)}, u32[]{:S(2)}, u32[]{:S(2)}) collective-permute-start(bf16[896,256]{1,0:T(8,128)(2,1)S(1)} %slice.65), channel_id=1, source_target_pairs={{0,4},{4,8},{8,12},{12,16},{16,20},{20,24},{24,28},{1,5},{5,9},{9,... | collective-permute-start | bytes 1376264 | tf_op jit(solution)/shard_map/ppermute | solution.py:132
  196.4 8.8 %collective-permute-done.6 = bf16[896,256]{1,0:T(8,128)(2,1)S(1)} collective-permute-done((bf16[896,256]{1,0:T(8,128)(2,1)S(1)}, bf16[896,256]{1,0:T(8,128)(2,1)S(1)}, u32[]{:S(2)}, u32[]{:S(2)}) %collective-permute-start.6) | collective-permute-done | bytes 458784 | tf_op jit(solution)/shard_map/ppermute | solution.py:132
  206.4 17.1 %attend.6 = bf16[16,128,512]{2,1,0:T(8,128)(2,1)} custom-call(s32[16]{0:T(128)} %reduce_sum.40.block_ref, s32[16]{0:T(128)} %select_reduce_fusion.count_ref, bf16[2048,512]{1,0:T(8,128)(2,1)} %slice.67.q_ref, bf16[2944,256]{1,0:T(8,128)(2,1)} %pad_maximum_fusion.kv_ref), custom_call_target="tpu_custom_call" | custom-call | flops 2684354560 | bytes 5701632 | tf_op jit(solution)/shard_map/attend/pallas_call | solution.py:74
  224.8 9.4 %all-to-all-start.1 = ((bf16[16,128,512]{2,1,0:T(8,128)(2,1)}), bf16[16,128,512]{2,1,0:T(8,128)(2,1)}, u32[]{:S(2)}, u32[]{:S(2)}) async-start(bf16[16,128,512]{2,1,0:T(8,128)(2,1)} %attend.6), calls=%async_computation.1 | async-start | bytes 4194304 | tf_op jit(solution)/shard_map/all_to_all | solution.py:241
  238.4 10.8 %collective-permute-done.1 = bf16[512,512]{1,0:T(8,128)(2,1)} collective-permute-done((bf16[512,512]{1,0:T(8,128)(2,1)S(1)}, bf16[512,512]{1,0:T(8,128)(2,1)}, u32[]{:S(2)}, u32[]{:S(2)}) %collective-permute-start.1) | collective-permute-done | bytes 524320 | tf_op jit(solution)/shard_map/ppermute | solution.py:179
  250.3 9.1 %collective-permute-done.2 = bf16[512,512]{1,0:T(8,128)(2,1)} collective-permute-done((bf16[512,512]{1,0:T(8,128)(2,1)S(1)}, bf16[512,512]{1,0:T(8,128)(2,1)}, u32[]{:S(2)}, u32[]{:S(2)}) %collective-permute-start.2) | collective-permute-done | bytes 524320 | tf_op jit(solution)/shard_map/ppermute | solution.py:179
  261.7 17.1 %attend.5 = bf16[16,128,512]{2,1,0:T(8,128)(2,1)} custom-call(s32[16]{0:T(128)} %reduce_sum.40.block_ref, s32[16]{0:T(128)} %select_reduce_fusion.count_ref, bf16[2048,512]{1,0:T(8,128)(2,1)} %copy-done.8, bf16[2944,256]{1,0:T(8,128)(2,1)} %pad_maximum_fusion.kv_ref), custom_call_target="tpu_custom_call" | custom-call | flops 2684354560 | bytes 5701632 | tf_op jit(solution)/shard_map/attend/pallas_call | solution.py:74
  278.8 4.8 %all-to-all-done.1.x_ref = bf16[16,128,512]{2,1,0:T(8,128)(2,1)} async-done(((bf16[16,128,512]{2,1,0:T(8,128)(2,1)}), bf16[16,128,512]{2,1,0:T(8,128)(2,1)}, u32[]{:S(2)}, u32[]{:S(2)}) %all-to-all-start.1) | async-done | bytes 2097184 | tf_op jit(solution)/shard_map/all_to_all | solution.py:241
  283.6 3.6 %all-to-all-start = ((bf16[16,128,512]{2,1,0:T(8,128)(2,1)}), bf16[16,128,512]{2,1,0:T(8,128)(2,1)S(1)}, u32[]{:S(2)}, u32[]{:S(2)}) async-start(bf16[16,128,512]{2,1,0:T(8,128)(2,1)} %attend.5), calls=%async_computation | async-start | bytes 4194304 | tf_op jit(solution)/shard_map/all_to_all | solution.py:241
  292.5 3.0 place.7.rest_0_
  295.6 3.0 place.8.rest_0_
  298.6 36.7 %all-to-all-done.x_ref = bf16[16,128,512]{2,1,0:T(8,128)(2,1)S(1)} async-done(((bf16[16,128,512]{2,1,0:T(8,128)(2,1)}), bf16[16,128,512]{2,1,0:T(8,128)(2,1)S(1)}, u32[]{:S(2)}, u32[]{:S(2)}) %all-to-all-start) | async-done | bytes 2097184 | tf_op jit(solution)/shard_map/all_to_all | solution.py:241
  336.6 3.0 place.9
  (114 shorter events, 52.0 us)
Async XLA Ops:
  3.9 18.7 %all-to-all-start.2 = ((bf16[4,512,256]{2,1,0:T(8,128)(2,1)}), bf16[4,512,256]{2,1,0:T(8,128)(2,1)S(1)}, u32[]{:S(2)}, u32[]{:S(2)}) async-start(bf16[4,512,256]{2,1,0:T(8,128)(2,1)} %pad_maximum_fusion.2), calls=%async_computation.2 | async-start | bytes 2097152 | tf_op jit(solution)/shard_map/all_to_all | solution.py:161
  22.6 21.4 %all-to-all-start.5 = ((bf16[4,512,256]{2,1,0:T(8,128)(2,1)}), bf16[4,512,256]{2,1,0:T(8,128)(2,1)S(1)}, u32[]{:S(2)}, u32[]{:S(2)}) async-start(bf16[4,512,256]{2,1,0:T(8,128)(2,1)} %pad_maximum_fusion.3), calls=%async_computation.5 | async-start | bytes 2097152 | tf_op jit(solution)/shard_map/all_to_all | solution.py:161
  26.9 14.8 %collective-permute-start.10 = (bf16[896,256]{1,0:T(8,128)(2,1)}, bf16[896,256]{1,0:T(8,128)(2,1)}, u32[]{:S(2)}, u32[]{:S(2)}) collective-permute-start(bf16[896,256]{1,0:T(8,128)(2,1)} %slice.68), channel_id=1, source_target_pairs={{0,4},{4,8},{8,12},{12,16},{16,20},{20,24},{24,28},{1,5},{5,9},{9,... | collective-permute-start | bytes 1376264 | tf_op jit(solution)/shard_map/ppermute | solution.py:132
  56.0 7.2 %copy-start.16 = (bf16[512,256]{1,0:T(8,128)(2,1)S(1)}, bf16[512,256]{1,0:T(8,128)(2,1)}, u32[]{:S(2)}) copy-start(bf16[512,256]{1,0:T(8,128)(2,1)} %get-tuple-element.11) | copy-start | bytes 786436
  56.0 7.3 %copy-start.15 = (bf16[512,256]{1,0:T(8,128)(2,1)S(1)}, bf16[512,256]{1,0:T(8,128)(2,1)}, u32[]{:S(2)}) copy-start(bf16[512,256]{1,0:T(8,128)(2,1)} %get-tuple-element.10) | copy-start | bytes 786436
  56.0 9.0 %copy-start.14 = (bf16[512,256]{1,0:T(8,128)(2,1)S(1)}, bf16[512,256]{1,0:T(8,128)(2,1)}, u32[]{:S(2)}) copy-start(bf16[512,256]{1,0:T(8,128)(2,1)} %get-tuple-element.9) | copy-start | bytes 786436
  56.0 33.2 %all-to-all-start.6 = ((bf16[16,128,256]{2,1,0:T(8,128)(2,1)}), bf16[16,128,256]{2,1,0:T(8,128)(2,1)S(1)}, u32[]{:S(2)}, u32[]{:S(2)}) async-start(bf16[16,128,256]{2,1,0:T(8,128)(2,1)} %attend.9), calls=%async_computation.6 | async-start | bytes 2097152 | tf_op jit(solution)/shard_map/all_to_all | solution.py:241
  63.3 1.9 collective-permute-start.11
  63.3 9.3 %collective-permute-start.12 = (bf16[512,256]{1,0:T(8,128)(2,1)S(1)}, bf16[512,256]{1,0:T(8,128)(2,1)}, u32[]{:S(2)}, u32[]{:S(2)}) collective-permute-start(bf16[512,256]{1,0:T(8,128)(2,1)S(1)} %copy-done.15), channel_id=1, source_target_pairs={{0,2},{1,3},{2,0},{3,1},{4,6},{5,7},{6,4},{7,5},{8,10},{9,11},{10,... | collective-permute-start | bytes 786440 | tf_op jit(solution)/shard_map/ppermute | solution.py:179
  65.0 12.1 %collective-permute-start.13 = (bf16[512,256]{1,0:T(8,128)(2,1)S(1)}, bf16[512,256]{1,0:T(8,128)(2,1)S(1)}, u32[]{:S(2)}, u32[]{:S(2)}) collective-permute-start(bf16[512,256]{1,0:T(8,128)(2,1)S(1)} %copy-done.14), channel_id=1, source_target_pairs={{0,3},{1,2},{2,1},{3,0},{4,7},{5,6},{6,5},{7,4},{8,11},{9,10},{10,... | collective-permute-start | bytes 786440 | tf_op jit(solution)/shard_map/ppermute | solution.py:179
  89.2 7.7 %copy-start.2 = (bf16[16,128,256]{2,1,0:T(8,128)(2,1)}, bf16[16,128,256]{2,1,0:T(8,128)(2,1)S(1)}, u32[]{:S(2)}) copy-start(bf16[16,128,256]{2,1,0:T(8,128)(2,1)S(1)} %all-to-all-done.6.x_ref) | copy-start | bytes 3145732
  89.2 55.3 %all-to-all-start.4 = ((bf16[16,128,256]{2,1,0:T(8,128)(2,1)}), bf16[16,128,256]{2,1,0:T(8,128)(2,1)S(1)}, u32[]{:S(2)}, u32[]{:S(2)}) async-start(bf16[16,128,256]{2,1,0:T(8,128)(2,1)} %attend.8), calls=%async_computation.4 | async-start | bytes 2097152 | tf_op jit(solution)/shard_map/all_to_all | solution.py:241
  101.6 1.9 collective-permute-start.7
  101.7 14.8 %collective-permute-start.8 = (bf16[512,512]{1,0:T(8,128)(2,1)S(1)}, bf16[512,512]{1,0:T(8,128)(2,1)S(1)}, u32[]{:S(2)}, u32[]{:S(2)}) collective-permute-start(bf16[512,512]{1,0:T(8,128)(2,1)S(1)} %get-tuple-element.16), channel_id=1, source_target_pairs={{0,2},{1,3},{2,0},{3,1},{4,6},{5,7},{6,4},{7,5},{8,10},{9,11},{10,... | collective-permute-start | bytes 1572872 | tf_op jit(solution)/shard_map/ppermute | solution.py:179
  103.3 23.3 %collective-permute-start.9 = (bf16[512,512]{1,0:T(8,128)(2,1)S(1)}, bf16[512,512]{1,0:T(8,128)(2,1)S(1)}, u32[]{:S(2)}, u32[]{:S(2)}) collective-permute-start(bf16[512,512]{1,0:T(8,128)(2,1)S(1)} %get-tuple-element.15), channel_id=1, source_target_pairs={{0,3},{1,2},{2,1},{3,0},{4,7},{5,6},{6,5},{7,4},{8,11},{9,10},{10,... | collective-permute-start | bytes 1572872 | tf_op jit(solution)/shard_map/ppermute | solution.py:179
  144.5 7.5 %copy-start.6 = (bf16[512,512]{1,0:T(8,128)(2,1)S(1)}, bf16[512,512]{1,0:T(8,128)(2,1)}, u32[]{:S(2)}) copy-start(bf16[512,512]{1,0:T(8,128)(2,1)} %get-tuple-element.21) | copy-start | bytes 1572868
  144.5 8.8 %copy-start.5 = (bf16[512,512]{1,0:T(8,128)(2,1)S(1)}, bf16[512,512]{1,0:T(8,128)(2,1)}, u32[]{:S(2)}) copy-start(bf16[512,512]{1,0:T(8,128)(2,1)} %get-tuple-element.20) | copy-start | bytes 1572868
  145.5 78.0 %all-to-all-start.3 = ((bf16[16,128,512]{2,1,0:T(8,128)(2,1)}), bf16[16,128,512]{2,1,0:T(8,128)(2,1)S(1)}, u32[]{:S(2)}, u32[]{:S(2)}) async-start(bf16[16,128,512]{2,1,0:T(8,128)(2,1)} %attend.7), calls=%async_computation.3 | async-start | bytes 4194304 | tf_op jit(solution)/shard_map/all_to_all | solution.py:241
  152.0 4.0 %copy-start.4 = (bf16[512,512]{1,0:T(8,128)(2,1)S(1)}, bf16[512,512]{1,0:T(8,128)(2,1)}, u32[]{:S(2)}) copy-start(bf16[512,512]{1,0:T(8,128)(2,1)} %get-tuple-element.19) | copy-start | bytes 1572868
  152.0 4.0 %copy-start.13 = (bf16[512,128]{1,0:T(8,128)(2,1)S(1)}, bf16[512,128]{1,0:T(8,128)(2,1)}, u32[]{:S(2)}) copy-start(bf16[512,128]{1,0:T(8,128)(2,1)} %get-tuple-element.47) | copy-start | bytes 393220
  153.1 4.0 %collective-permute-start.3 = (bf16[512,768]{1,0:T(8,128)(2,1)S(1)}, bf16[512,768]{1,0:T(8,128)(2,1)S(1)}, u32[]{:S(2)}, u32[]{:S(2)}) collective-permute-start(bf16[512,768]{1,0:T(8,128)(2,1)S(1)} %pad_maximum_fusion.4), channel_id=1, source_target_pairs={{0,1},{1,0},{2,3},{3,2},{4,5},{5,4},{6,7},{7,6},{8,9},{9,8},{10,11... | collective-permute-start | bytes 2359304 | tf_op jit(solution)/shard_map/ppermute | solution.py:179
  154.3 20.5 %collective-permute-start.4 = (bf16[512,768]{1,0:T(8,128)(2,1)S(1)}, bf16[512,768]{1,0:T(8,128)(2,1)S(1)}, u32[]{:S(2)}, u32[]{:S(2)}) collective-permute-start(bf16[512,768]{1,0:T(8,128)(2,1)S(1)} %pad_maximum_fusion.5), channel_id=1, source_target_pairs={{0,2},{1,3},{2,0},{3,1},{4,6},{5,7},{6,4},{7,5},{8,10},{9,11},{10,... | collective-permute-start | bytes 2359304 | tf_op jit(solution)/shard_map/ppermute | solution.py:179
  156.1 34.5 %collective-permute-start.5 = (bf16[512,768]{1,0:T(8,128)(2,1)S(1)}, bf16[512,768]{1,0:T(8,128)(2,1)S(1)}, u32[]{:S(2)}, u32[]{:S(2)}) collective-permute-start(bf16[512,768]{1,0:T(8,128)(2,1)S(1)} %pad_maximum_fusion.6), channel_id=1, source_target_pairs={{0,3},{1,2},{2,1},{3,0},{4,7},{5,6},{6,5},{7,4},{8,11},{9,10},{10,... | collective-permute-start | bytes 2359304 | tf_op jit(solution)/shard_map/ppermute | solution.py:179
  190.7 14.5 %collective-permute-start.6 = (bf16[896,256]{1,0:T(8,128)(2,1)S(1)}, bf16[896,256]{1,0:T(8,128)(2,1)S(1)}, u32[]{:S(2)}, u32[]{:S(2)}) collective-permute-start(bf16[896,256]{1,0:T(8,128)(2,1)S(1)} %slice.65), channel_id=1, source_target_pairs={{0,4},{4,8},{8,12},{12,16},{16,20},{20,24},{24,28},{1,5},{5,9},{9,... | collective-permute-start | bytes 1376264 | tf_op jit(solution)/shard_map/ppermute | solution.py:132
  223.5 10.7 %copy-start.12 = (bf16[512,512]{1,0:T(8,128)(2,1)S(1)}, bf16[512,512]{1,0:T(8,128)(2,1)}, u32[]{:S(2)}) copy-start(bf16[512,512]{1,0:T(8,128)(2,1)} %get-tuple-element.24) | copy-start | bytes 1572868
  223.5 12.4 %copy-start.11 = (bf16[512,512]{1,0:T(8,128)(2,1)S(1)}, bf16[512,512]{1,0:T(8,128)(2,1)}, u32[]{:S(2)}) copy-start(bf16[512,512]{1,0:T(8,128)(2,1)} %get-tuple-element.23) | copy-start | bytes 1572868
  224.8 58.8 %all-to-all-start.1 = ((bf16[16,128,512]{2,1,0:T(8,128)(2,1)}), bf16[16,128,512]{2,1,0:T(8,128)(2,1)}, u32[]{:S(2)}, u32[]{:S(2)}) async-start(bf16[16,128,512]{2,1,0:T(8,128)(2,1)} %attend.6), calls=%async_computation.1 | async-start | bytes 4194304 | tf_op jit(solution)/shard_map/all_to_all | solution.py:241
  234.2 3.1 collective-permute-start
  234.2 15.0 %collective-permute-start.1 = (bf16[512,512]{1,0:T(8,128)(2,1)S(1)}, bf16[512,512]{1,0:T(8,128)(2,1)}, u32[]{:S(2)}, u32[]{:S(2)}) collective-permute-start(bf16[512,512]{1,0:T(8,128)(2,1)S(1)} %copy-done.12), channel_id=1, source_target_pairs={{0,2},{1,3},{2,0},{3,1},{4,6},{5,7},{6,4},{7,5},{8,10},{9,11},{10,... | collective-permute-start | bytes 1572872 | tf_op jit(solution)/shard_map/ppermute | solution.py:179
  235.9 23.4 %collective-permute-start.2 = (bf16[512,512]{1,0:T(8,128)(2,1)S(1)}, bf16[512,512]{1,0:T(8,128)(2,1)}, u32[]{:S(2)}, u32[]{:S(2)}) collective-permute-start(bf16[512,512]{1,0:T(8,128)(2,1)S(1)} %copy-done.11), channel_id=1, source_target_pairs={{0,3},{1,2},{2,1},{3,0},{4,7},{5,6},{6,5},{7,4},{8,11},{9,10},{10,... | collective-permute-start | bytes 1572872 | tf_op jit(solution)/shard_map/ppermute | solution.py:179
  283.6 51.7 %all-to-all-start = ((bf16[16,128,512]{2,1,0:T(8,128)(2,1)}), bf16[16,128,512]{2,1,0:T(8,128)(2,1)S(1)}, u32[]{:S(2)}, u32[]{:S(2)}) async-start(bf16[16,128,512]{2,1,0:T(8,128)(2,1)} %attend.5), calls=%async_computation | async-start | bytes 4194304 | tf_op jit(solution)/shard_map/all_to_all | solution.py:241
  335.3 1.4 copy-start.1
  (8 other events, 8.9 us)
where the time goes:
time: 341 us; the launch traced here: 340 us
  waiting for transfers between devices  148 us (43%)
  Pallas kernels  87.2 us (26%)
  starting transfers between devices  57.4 us (17%)
  local copies, waits for them, and re-layouts  34.5 us (10%)
  other arithmetic  12.4 us (4%)
    ppermute x12, waiting for transfers between devices, by_permutes(): lax.ppermute(piece, 'head', [(h, h ^ step) for h in range(head_count)])  84.6 us
    pallas_call x5, Pallas kernels, attend(): pl.pallas_call(functools.partial(attend_kernel, heads), out_shape=jax.Sha...  73.4 us
    all_to_all x5, waiting for transfers between devices, shards(): lax.all_to_all(out, 'ctx', split_axis=0, concat_axis=0, tiled=True)  41.5 us
    all_to_all x5, starting transfers between devices, shards(): lax.all_to_all(out, 'ctx', split_axis=0, concat_axis=0, tiled=True)  32.9 us
    pallas_call x5, Pallas kernels, place(): pl.pallas_call(functools.partial(place_kernel, first), out_shape=jax.Shap...  13.8 us
    ppermute x2, waiting for transfers between devices, shifted(): return lax.ppermute(shard, axis, pairs)  12.4 us
    all_to_all x2, waiting for transfers between devices, all_pairs(): lax.all_to_all(parts, 'head', split_axis=0, concat_axis=0, tiled=True)  9.27 us
    ppermute x2, starting transfers between devices, shifted(): return lax.ppermute(shard, axis, pairs)  9.04 us
  transfers between devices with their start and end apart: 21, of which 13 were waited for; matrix products, arithmetic and copies ran while one was open for 10% of the time, Pallas kernels for 21%

commit v1 on v0

--- a/solution.py
+++ b/solution.py
@@ -28,15 +28,21 @@
         keys = kv_ref[pl.ds(first, width), :HD]
         values = kv_ref[pl.ds(first, width), HD:]
         inside = jnp.full((rows, BLK), count - (2 * pairs - 1), jnp.int32) > 0
+        all_scores = []
         for step in range(heads // ROW_HEADS):
             base = step * ROW_HEADS * HD
             queries = jnp.concatenate(
                 [q_ref[q_rows, base + i * HD : base + (i + 1) * HD] for i in range(ROW_HEADS)],
                 axis=0,
             )
-            scores = lax.dot_general(
-                queries, keys, (((1,), (1,)), ((), ())), preferred_element_type=jnp.float32
-            )
+            all_scores.append(
+                lax.dot_general(
+                    queries, keys, (((1,), (1,)), ((), ())), preferred_element_type=jnp.float32
+                )
+            )
+        for step in range(heads // ROW_HEADS):
+            base = step * ROW_HEADS * HD
+            scores = all_scores[step]
             parts = [scores[:, i * BLK : (i + 1) * BLK] for i in range(2 * pairs)]
             parts[0] = jnp.where(inside, parts[0], -jnp.inf)
             parts[-1] = jnp.where(causal, parts[-1], -jnp.inf)
@@ -144,10 +150,10 @@
     group = q_width // HD // kv_heads
     head = lax.axis_index("head")
 
-    def pieces(kv_head, first, heads, with_kv, of_head):
+    def pieces(first, heads, fresh, of_head):
         wanted = [(query, of_head * q_width + first * HD, heads * HD)]
-        if with_kv:
-            start = of_head * kv_width + kv_head * HD
+        if fresh is not None:
+            start = of_head * kv_width + fresh * HD
             wanted += [(key, start, HD), (value, start, HD)]
         return wanted
 
@@ -217,27 +223,29 @@
     for kv_head in range(kv_heads):
         sizes = [group // 4, group // 4, group // 2] if kv_head == 0 else [group // 2] * 2
         start = kv_head * group
-        for i, size in enumerate(sizes):
-            chunks.append((kv_head, start, size, i == 0))
+        for size in sizes:
+            chunks.append((kv_head, start, size))
             start += size
 
-    result = None
-    window = None
+    windows = {}
     arrived = []
-    for at, (kv_head, first, heads, fresh) in enumerate(chunks):
+    for at, (kv_head, first, heads) in enumerate(chunks):
+        fresh = at if at < kv_heads else None
         if at == 0:
             kv = all_pairs(
                 lambda h: [(x, h * kv_width, HD) for x in (key, value)]
             )
             q = all_pairs(lambda h: [(query, h * q_width, heads * HD)])
         else:
-            both = by_permutes(functools.partial(pieces, kv_head, first, heads, fresh))
+            both = by_permutes(functools.partial(pieces, first, heads, fresh))
             q = both[:, : heads * HD]
             kv = both[:, heads * HD :]
-        arrived.append((kv_head, first, heads, q, windowed(kv) if fresh else None))
-    for kv_head, first, heads, q, fresh_window in arrived:
-        window = window if fresh_window is None else fresh_window
-        out = attend(slot_block, slot_count, q, window)
+        if fresh is not None:
+            windows[fresh] = windowed(kv)
+        arrived.append(q)
+    result = None
+    for at, (kv_head, first, heads) in enumerate(chunks):
+        out = attend(slot_block, slot_count, arrived[at], windows[kv_head])
         received = lax.all_to_all(out, "ctx", split_axis=0, concat_axis=0, tiled=True)
         result = place(mine, received, result, first * HD, q_width)
     return result

time: 341 us -> 325 us (0.953)
  Pallas kernels: 87.2 us -> 76.4 us
  starting transfers between devices: 57.4 us -> 52.5 us
    all_to_all x5, waiting for transfers between devices: 41.5 us -> 53 us  [shards(): lax.all_to_all(out, 'ctx', split_axis=0, concat_axis=0, tiled=True)]
    pallas_call x5, Pallas kernels: 73.4 us -> 62.7 us  [attend(): pl.pallas_call(functools.partial(attend_kernel, heads), out_shape=jax.Sha...]
    ppermute x12, waiting for transfers between devices: 84.6 us -> 76.9 us  [by_permutes(): lax.ppermute(piece, 'head', [(h, h ^ step) for h in range(head_count)])]
    dynamic_update_slice x13 -> x14, local copies, waits for them, and re-layouts: 8.94 us -> 14.5 us  [by_permutes(): whole = lax.dynamic_update_slice(whole, piece, (other * local_rows, 0))]
    ppermute x2, waiting for transfers between devices: 12.4 us -> 7.44 us  [shifted(): return lax.ppermute(shard, axis, pairs)]
    all_to_all x5, starting transfers between devices: 32.9 us -> 28.4 us  [shards(): lax.all_to_all(out, 'ctx', split_axis=0, concat_axis=0, tiled=True)]
    unnamed x38 -> x40, local copies, waits for them, and re-layouts: 7.5 us -> 6.84 us
  transfers between devices with their start and end apart: 21 -> 21, of which waited for: 13 -> 14; matrix products, arithmetic and copies ran while one was open for 10% -> 11% of each run, Pallas kernels for 21% -> 19%
where the time goes in v1:
time: 325 us; the launch traced here: 324 us
  waiting for transfers between devices  149 us (46%)
  Pallas kernels  76.4 us (24%)
  starting transfers between devices  52.5 us (16%)
  local copies, waits for them, and re-layouts  34.7 us (11%)
  other arithmetic  11.3 us (3%)
    ppermute x12, waiting for transfers between devices, by_permutes(): lax.ppermute(piece, 'head', [(h, h ^ step) for h in range(head_count)])  76.9 us
    pallas_call x5, Pallas kernels, attend(): pl.pallas_call(functools.partial(attend_kernel, heads), out_shape=jax.Sha...  62.7 us
    all_to_all x5, waiting for transfers between devices, shards(): lax.all_to_all(out, 'ctx', split_axis=0, concat_axis=0, tiled=True)  53 us
    all_to_all x5, starting transfers between devices, shards(): lax.all_to_all(out, 'ctx', split_axis=0, concat_axis=0, tiled=True)  28.4 us
    dynamic_update_slice x14, local copies, waits for them, and re-layouts, by_permutes(): whole = lax.dynamic_update_slice(whole, piece, (other * local_rows, 0))  14.5 us
    pallas_call x5, Pallas kernels, place(): pl.pallas_call(functools.partial(place_kernel, first), out_shape=jax.Shap...  13.8 us
    all_to_all x2, waiting for transfers between devices, all_pairs(): lax.all_to_all(parts, 'head', split_axis=0, concat_axis=0, tiled=True)  11.3 us
    ppermute x2, starting transfers between devices, shifted(): return lax.ppermute(shard, axis, pairs)  8.81 us
  transfers between devices with their start and end apart: 21, of which 14 were waited for; matrix products, arithmetic and copies ran while one was open for 11% of the time, Pallas kernels for 19%

profile of v1, /device:TPU:0, one launch (start us, length us, event | category | flops | bytes accessed | tf_op | source)
XLA Modules:
  0.0 324.1 jit_solution(6727443602057187234)
XLA Ops:
  0.0 2.6 fusion.6
  3.9 4.3 %all-to-all-start.2 = ((bf16[4,512,256]{2,1,0:T(8,128)(2,1)}), bf16[4,512,256]{2,1,0:T(8,128)(2,1)S(1)}, u32[]{:S(2)}, u32[]{:S(2)}) async-start(bf16[4,512,256]{2,1,0:T(8,128)(2,1)} %pad_maximum_fusion.2), calls=%async_computation.2 | async-start | bytes 2097152 | tf_op jit(solution)/shard_map/all_to_all | solution.py:167
  11.3 11.3 %all-to-all-done.2 = bf16[4,512,256]{2,1,0:T(8,128)(2,1)S(1)} async-done(((bf16[4,512,256]{2,1,0:T(8,128)(2,1)}), bf16[4,512,256]{2,1,0:T(8,128)(2,1)S(1)}, u32[]{:S(2)}, u32[]{:S(2)}) %all-to-all-start.2) | async-done | bytes 1048608 | tf_op jit(solution)/shard_map/all_to_all | solution.py:167
  22.6 3.5 %all-to-all-start.5 = ((bf16[4,512,256]{2,1,0:T(8,128)(2,1)}), bf16[4,512,256]{2,1,0:T(8,128)(2,1)S(1)}, u32[]{:S(2)}, u32[]{:S(2)}) async-start(bf16[4,512,256]{2,1,0:T(8,128)(2,1)} %pad_maximum_fusion.3), calls=%async_computation.5 | async-start | bytes 2097152 | tf_op jit(solution)/shard_map/all_to_all | solution.py:167
  26.9 4.9 %collective-permute-start.13 = (bf16[896,256]{1,0:T(8,128)(2,1)}, bf16[896,256]{1,0:T(8,128)(2,1)}, u32[]{:S(2)}, u32[]{:S(2)}) collective-permute-start(bf16[896,256]{1,0:T(8,128)(2,1)} %slice.67), channel_id=1, source_target_pairs={{0,4},{4,8},{8,12},{12,16},{16,20},{20,24},{24,28},{1,5},{5,9},{9,... | collective-permute-start | bytes 1376264 | tf_op jit(solution)/shard_map/ppermute | solution.py:138
  34.3 7.4 %collective-permute-done.13 = bf16[896,256]{1,0:T(8,128)(2,1)} collective-permute-done((bf16[896,256]{1,0:T(8,128)(2,1)}, bf16[896,256]{1,0:T(8,128)(2,1)}, u32[]{:S(2)}, u32[]{:S(2)}) %collective-permute-start.13) | collective-permute-done | bytes 458784 | tf_op jit(solution)/shard_map/ppermute | solution.py:138
  44.9 11.1 %attend.9 = bf16[16,128,256]{2,1,0:T(8,128)(2,1)} custom-call(s32[16]{0:T(128)} %reduce_sum.40.block_ref, s32[16]{0:T(128)} %select_reduce_fusion.count_ref, bf16[2048,256]{1,0:T(8,128)(2,1)} %bitcast.24, bf16[2944,256]{1,0:T(8,128)(2,1)} %pad_maximum_fusion.1.kv_ref), custom_call_target="tpu_custom_call" | custom-call | flops 1342177280 | bytes 3604480 | tf_op jit(solution)/shard_map/attend/pallas_call | solution.py:80
  56.1 7.2 %all-to-all-start.6 = ((bf16[16,128,256]{2,1,0:T(8,128)(2,1)}), bf16[16,128,256]{2,1,0:T(8,128)(2,1)S(1)}, u32[]{:S(2)}, u32[]{:S(2)}) async-start(bf16[16,128,256]{2,1,0:T(8,128)(2,1)} %attend.9), calls=%async_computation.6 | async-start | bytes 2097152 | tf_op jit(solution)/shard_map/all_to_all | solution.py:249
  69.9 10.2 %collective-permute-done.4 = bf16[512,512]{1,0:T(8,128)(2,1)} collective-permute-done((bf16[512,512]{1,0:T(8,128)(2,1)}, bf16[512,512]{1,0:T(8,128)(2,1)}, u32[]{:S(2)}, u32[]{:S(2)}) %collective-permute-start.4) | collective-permute-done | bytes 524320 | tf_op jit(solution)/shard_map/ppermute | solution.py:185
  81.2 9.2 %collective-permute-done.5 = bf16[512,512]{1,0:T(8,128)(2,1)} collective-permute-done((bf16[512,512]{1,0:T(8,128)(2,1)}, bf16[512,512]{1,0:T(8,128)(2,1)}, u32[]{:S(2)}, u32[]{:S(2)}) %collective-permute-start.5) | collective-permute-done | bytes 524320 | tf_op jit(solution)/shard_map/ppermute | solution.py:185
  93.1 11.1 %attend.8 = bf16[16,128,256]{2,1,0:T(8,128)(2,1)} custom-call(s32[16]{0:T(128)} %reduce_sum.40.block_ref, s32[16]{0:T(128)} %select_reduce_fusion.count_ref, bf16[2048,256]{1,0:T(8,128)(2,1)} %get-tuple-element.25.q_ref, bf16[2944,256]{1,0:T(8,128)(2,1)} %pad_maximum_fusion.1.kv_ref), custom_call_target="tpu_custom_call" | custom-call | flops 1342177280 | bytes 3604480 | tf_op jit(solution)/shard_map/attend/pallas_call | solution.py:80
  104.2 6.3 %all-to-all-start.4 = ((bf16[16,128,256]{2,1,0:T(8,128)(2,1)}), bf16[16,128,256]{2,1,0:T(8,128)(2,1)}, u32[]{:S(2)}, u32[]{:S(2)}) async-start(bf16[16,128,256]{2,1,0:T(8,128)(2,1)} %attend.8), calls=%async_computation.4 | async-start | bytes 2097152 | tf_op jit(solution)/shard_map/all_to_all | solution.py:249
  110.6 4.8 %constant_dynamic-slice_fusion.5 = (bf16[512,512]{1,0:T(8,128)(2,1)}, bf16[512,512]{1,0:T(8,128)(2,1)}, bf16[512,512]{1,0:T(8,128)(2,1)}, bf16[2048,512]{1,0:T(8...) fusion(bf16[512,8192]{1,0:T(8,128)(2,1)} %param.5, ...), kind=kLoop, calls=%fused_computation.35 | loop fusion | bytes 10485804 | tf_op jit(solution)/shard_map/dynamic_slice | solution.py:174
  118.6 4.0 %collective-permute-start.6 = (bf16[896,256]{1,0:T(8,128)(2,1)S(1)}, bf16[896,256]{1,0:T(8,128)(2,1)S(1)}, u32[]{:S(2)}, u32[]{:S(2)}) collective-permute-start(bf16[896,256]{1,0:T(8,128)(2,1)S(1)} %slice.65), channel_id=1, source_target_pairs={{0,4},{4,8},{8,12},{12,16},{16,20},{20,24},{24,28},{1,5},{5,9},{9,... | collective-permute-start | bytes 1376264 | tf_op jit(solution)/shard_map/ppermute | solution.py:138
  125.0 6.8 %collective-permute-done.8 = bf16[512,512]{1,0:T(8,128)(2,1)} collective-permute-done((bf16[512,512]{1,0:T(8,128)(2,1)}, bf16[512,512]{1,0:T(8,128)(2,1)}, u32[]{:S(2)}, u32[]{:S(2)}) %collective-permute-start.8) | collective-permute-done | bytes 524320 | tf_op jit(solution)/shard_map/ppermute | solution.py:185
  132.9 9.2 %collective-permute-done.9 = bf16[512,512]{1,0:T(8,128)(2,1)} collective-permute-done((bf16[512,512]{1,0:T(8,128)(2,1)}, bf16[512,512]{1,0:T(8,128)(2,1)}, u32[]{:S(2)}, u32[]{:S(2)}) %collective-permute-start.9) | collective-permute-done | bytes 524320 | tf_op jit(solution)/shard_map/ppermute | solution.py:185
  145.0 13.5 %attend.6 = bf16[16,128,512]{2,1,0:T(8,128)(2,1)} custom-call(s32[16]{0:T(128)} %reduce_sum.40.block_ref, s32[16]{0:T(128)} %select_reduce_fusion.count_ref, bf16[2048,512]{1,0:T(8,128)(2,1)} %copy-done.6, bf16[2944,256]{1,0:T(8,128)(2,1)} %pad_maximum_fusion.kv_ref), custom_call_target="tpu_custom_call" | custom-call | flops 2684354560 | bytes 5701632 | tf_op jit(solution)/shard_map/attend/pallas_call | solution.py:80
  158.5 6.9 %all-to-all-start.1 = ((bf16[16,128,512]{2,1,0:T(8,128)(2,1)}), bf16[16,128,512]{2,1,0:T(8,128)(2,1)S(1)}, u32[]{:S(2)}, u32[]{:S(2)}) async-start(bf16[16,128,512]{2,1,0:T(8,128)(2,1)} %attend.6), calls=%async_computation.1 | async-start | bytes 4194304 | tf_op jit(solution)/shard_map/all_to_all | solution.py:249
  168.4 11.9 %collective-permute-done.11 = bf16[512,512]{1,0:T(8,128)(2,1)S(1)} collective-permute-done((bf16[512,512]{1,0:T(8,128)(2,1)S(1)}, bf16[512,512]{1,0:T(8,128)(2,1)S(1)}, u32[]{:S(2)}, u32[]{:S(2)}) %collective-permute-start.11) | collective-permute-done | bytes 524320 | tf_op jit(solution)/shard_map/ppermute | solution.py:185
  181.1 9.3 %collective-permute-done.12 = bf16[512,512]{1,0:T(8,128)(2,1)S(1)} collective-permute-done((bf16[512,512]{1,0:T(8,128)(2,1)S(1)}, bf16[512,512]{1,0:T(8,128)(2,1)S(1)}, u32[]{:S(2)}, u32[]{:S(2)}) %collective-permute-start.12) | collective-permute-done | bytes 524320 | tf_op jit(solution)/shard_map/ppermute | solution.py:185
  191.3 13.4 %attend.7 = bf16[16,128,512]{2,1,0:T(8,128)(2,1)} custom-call(s32[16]{0:T(128)} %reduce_sum.40.block_ref, s32[16]{0:T(128)} %select_reduce_fusion.count_ref, bf16[2048,512]{1,0:T(8,128)(2,1)} %constant_dynamic-update-slice_fusion.1.q_ref, bf16[2944,256]{1,0:T(8,128)(2,1)} %pad_maximum_fusion.1.kv_ref), custom_call_target="tpu_custom_call" | custom-call | flops 2684354560 | bytes 5701632 | tf_op jit(solution)/shard_map/attend/pallas_call | solution.py:80
  204.8 9.2 %all-to-all-done.1.x_ref = bf16[16,128,512]{2,1,0:T(8,128)(2,1)S(1)} async-done(((bf16[16,128,512]{2,1,0:T(8,128)(2,1)}), bf16[16,128,512]{2,1,0:T(8,128)(2,1)S(1)}, u32[]{:S(2)}, u32[]{:S(2)}) %all-to-all-start.1) | async-done | bytes 2097184 | tf_op jit(solution)/shard_map/all_to_all | solution.py:249
  215.3 4.4 %all-to-all-start.3 = ((bf16[16,128,512]{2,1,0:T(8,128)(2,1)}), bf16[16,128,512]{2,1,0:T(8,128)(2,1)}, u32[]{:S(2)}, u32[]{:S(2)}) async-start(bf16[16,128,512]{2,1,0:T(8,128)(2,1)} %attend.7), calls=%async_computation.3 | async-start | bytes 4194304 | tf_op jit(solution)/shard_map/all_to_all | solution.py:249
  223.9 10.8 %collective-permute-done.1 = bf16[512,512]{1,0:T(8,128)(2,1)} collective-permute-done((bf16[512,512]{1,0:T(8,128)(2,1)S(1)}, bf16[512,512]{1,0:T(8,128)(2,1)}, u32[]{:S(2)}, u32[]{:S(2)}) %collective-permute-start.1) | collective-permute-done | bytes 524320 | tf_op jit(solution)/shard_map/ppermute | solution.py:185
  235.8 9.1 %collective-permute-done.2 = bf16[512,512]{1,0:T(8,128)(2,1)} collective-permute-done((bf16[512,512]{1,0:T(8,128)(2,1)S(1)}, bf16[512,512]{1,0:T(8,128)(2,1)}, u32[]{:S(2)}, u32[]{:S(2)}) %collective-permute-start.2) | collective-permute-done | bytes 524320 | tf_op jit(solution)/shard_map/ppermute | solution.py:185
  247.2 13.5 %attend.5 = bf16[16,128,512]{2,1,0:T(8,128)(2,1)} custom-call(s32[16]{0:T(128)} %reduce_sum.40.block_ref, s32[16]{0:T(128)} %select_reduce_fusion.count_ref, bf16[2048,512]{1,0:T(8,128)(2,1)} %copy-done.5, bf16[2944,256]{1,0:T(8,128)(2,1)} %pad_maximum_fusion.kv_ref), custom_call_target="tpu_custom_call" | custom-call | flops 2684354560 | bytes 5701632 | tf_op jit(solution)/shard_map/attend/pallas_call | solution.py:80
  260.8 6.7 %all-to-all-done.3.x_ref = bf16[16,128,512]{2,1,0:T(8,128)(2,1)} async-done(((bf16[16,128,512]{2,1,0:T(8,128)(2,1)}), bf16[16,128,512]{2,1,0:T(8,128)(2,1)}, u32[]{:S(2)}, u32[]{:S(2)}) %all-to-all-start.3) | async-done | bytes 2097184 | tf_op jit(solution)/shard_map/all_to_all | solution.py:249
  267.5 3.6 %all-to-all-start = ((bf16[16,128,512]{2,1,0:T(8,128)(2,1)}), bf16[16,128,512]{2,1,0:T(8,128)(2,1)S(1)}, u32[]{:S(2)}, u32[]{:S(2)}) async-start(bf16[16,128,512]{2,1,0:T(8,128)(2,1)} %attend.5), calls=%async_computation | async-start | bytes 4194304 | tf_op jit(solution)/shard_map/all_to_all | solution.py:249
  276.2 3.0 place.7.rest_0_
  279.3 3.0 place.8.rest_0_
  282.4 37.1 %all-to-all-done.x_ref = bf16[16,128,512]{2,1,0:T(8,128)(2,1)S(1)} async-done(((bf16[16,128,512]{2,1,0:T(8,128)(2,1)}), bf16[16,128,512]{2,1,0:T(8,128)(2,1)S(1)}, u32[]{:S(2)}, u32[]{:S(2)}) %all-to-all-start) | async-done | bytes 2097184 | tf_op jit(solution)/shard_map/all_to_all | solution.py:249
  320.9 3.0 place.9
  (116 shorter events, 51.0 us)
Async XLA Ops:
  3.9 18.7 %all-to-all-start.2 = ((bf16[4,512,256]{2,1,0:T(8,128)(2,1)}), bf16[4,512,256]{2,1,0:T(8,128)(2,1)S(1)}, u32[]{:S(2)}, u32[]{:S(2)}) async-start(bf16[4,512,256]{2,1,0:T(8,128)(2,1)} %pad_maximum_fusion.2), calls=%async_computation.2 | async-start | bytes 2097152 | tf_op jit(solution)/shard_map/all_to_all | solution.py:167
  22.6 21.4 %all-to-all-start.5 = ((bf16[4,512,256]{2,1,0:T(8,128)(2,1)}), bf16[4,512,256]{2,1,0:T(8,128)(2,1)S(1)}, u32[]{:S(2)}, u32[]{:S(2)}) async-start(bf16[4,512,256]{2,1,0:T(8,128)(2,1)} %pad_maximum_fusion.3), calls=%async_computation.5 | async-start | bytes 2097152 | tf_op jit(solution)/shard_map/all_to_all | solution.py:167
  26.9 14.8 %collective-permute-start.13 = (bf16[896,256]{1,0:T(8,128)(2,1)}, bf16[896,256]{1,0:T(8,128)(2,1)}, u32[]{:S(2)}, u32[]{:S(2)}) collective-permute-start(bf16[896,256]{1,0:T(8,128)(2,1)} %slice.67), channel_id=1, source_target_pairs={{0,4},{4,8},{8,12},{12,16},{16,20},{20,24},{24,28},{1,5},{5,9},{9,... | collective-permute-start | bytes 1376264 | tf_op jit(solution)/shard_map/ppermute | solution.py:138
  56.0 7.3 %copy-start.16 = (bf16[512,128]{1,0:T(8,128)(2,1)S(1)}, bf16[512,128]{1,0:T(8,128)(2,1)}, u32[]{:S(2)}) copy-start(bf16[512,128]{1,0:T(8,128)(2,1)} %get-tuple-element.31) | copy-start | bytes 393220
  56.0 7.3 %copy-start.17 = (bf16[512,128]{1,0:T(8,128)(2,1)S(1)}, bf16[512,128]{1,0:T(8,128)(2,1)}, u32[]{:S(2)}) copy-start(bf16[512,128]{1,0:T(8,128)(2,1)} %get-tuple-element.46) | copy-start | bytes 393220
  56.0 8.1 %copy-start.14 = (bf16[512,128]{1,0:T(8,128)(2,1)S(1)}, bf16[512,128]{1,0:T(8,128)(2,1)}, u32[]{:S(2)}) copy-start(bf16[512,128]{1,0:T(8,128)(2,1)} %get-tuple-element.30) | copy-start | bytes 393220
  56.1 8.1 %copy-start.15 = (bf16[512,128]{1,0:T(8,128)(2,1)S(1)}, bf16[512,128]{1,0:T(8,128)(2,1)}, u32[]{:S(2)}) copy-start(bf16[512,128]{1,0:T(8,128)(2,1)} %get-tuple-element.47) | copy-start | bytes 393220
  56.1 10.6 %copy-start.12 = (bf16[512,128]{1,0:T(8,128)(2,1)S(1)}, bf16[512,128]{1,0:T(8,128)(2,1)}, u32[]{:S(2)}) copy-start(bf16[512,128]{1,0:T(8,128)(2,1)} %get-tuple-element.29) | copy-start | bytes 393220
  56.1 10.6 %copy-start.13 = (bf16[512,128]{1,0:T(8,128)(2,1)S(1)}, bf16[512,128]{1,0:T(8,128)(2,1)}, u32[]{:S(2)}) copy-start(bf16[512,128]{1,0:T(8,128)(2,1)} %get-tuple-element.48) | copy-start | bytes 393220
  56.1 48.1 %all-to-all-start.6 = ((bf16[16,128,256]{2,1,0:T(8,128)(2,1)}), bf16[16,128,256]{2,1,0:T(8,128)(2,1)S(1)}, u32[]{:S(2)}, u32[]{:S(2)}) async-start(bf16[16,128,256]{2,1,0:T(8,128)(2,1)} %attend.9), calls=%async_computation.6 | async-start | bytes 2097152 | tf_op jit(solution)/shard_map/all_to_all | solution.py:249
  64.2 4.7 %collective-permute-start.3 = (bf16[512,512]{1,0:T(8,128)(2,1)}, bf16[512,512]{1,0:T(8,128)(2,1)}, u32[]{:S(2)}, u32[]{:S(2)}) collective-permute-start(bf16[512,512]{1,0:T(8,128)(2,1)} %pad_maximum_fusion.4), channel_id=1, source_target_pairs={{0,1},{1,0},{2,3},{3,2},{4,5},{5,4},{6,7},{7,6},{8,9},{9,8},{10,11... | collective-permute-start | bytes 1572872 | tf_op jit(solution)/shard_map/ppermute | solution.py:185
  65.0 15.1 %collective-permute-start.4 = (bf16[512,512]{1,0:T(8,128)(2,1)}, bf16[512,512]{1,0:T(8,128)(2,1)}, u32[]{:S(2)}, u32[]{:S(2)}) collective-permute-start(bf16[512,512]{1,0:T(8,128)(2,1)} %pad_maximum_fusion.5), channel_id=1, source_target_pairs={{0,2},{1,3},{2,0},{3,1},{4,6},{5,7},{6,4},{7,5},{8,10},{9,11},{10,... | collective-permute-start | bytes 1572872 | tf_op jit(solution)/shard_map/ppermute | solution.py:185
  67.5 22.9 %collective-permute-start.5 = (bf16[512,512]{1,0:T(8,128)(2,1)}, bf16[512,512]{1,0:T(8,128)(2,1)}, u32[]{:S(2)}, u32[]{:S(2)}) collective-permute-start(bf16[512,512]{1,0:T(8,128)(2,1)} %pad_maximum_fusion.6), channel_id=1, source_target_pairs={{0,3},{1,2},{2,1},{3,0},{4,7},{5,6},{6,5},{7,4},{8,11},{9,10},{10,... | collective-permute-start | bytes 1572872 | tf_op jit(solution)/shard_map/ppermute | solution.py:185
  104.2 54.4 %all-to-all-start.4 = ((bf16[16,128,256]{2,1,0:T(8,128)(2,1)}), bf16[16,128,256]{2,1,0:T(8,128)(2,1)}, u32[]{:S(2)}, u32[]{:S(2)}) async-start(bf16[16,128,256]{2,1,0:T(8,128)(2,1)} %attend.8), calls=%async_computation.4 | async-start | bytes 2097152 | tf_op jit(solution)/shard_map/all_to_all | solution.py:249
  116.7 7.2 %collective-permute-start.7 = (bf16[512,512]{1,0:T(8,128)(2,1)}, bf16[512,512]{1,0:T(8,128)(2,1)}, u32[]{:S(2)}, u32[]{:S(2)}) collective-permute-start(bf16[512,512]{1,0:T(8,128)(2,1)} %get-tuple-element.21), channel_id=1, source_target_pairs={{0,1},{1,0},{2,3},{3,2},{4,5},{5,4},{6,7},{7,6},{8,9},{9,8},{10,11... | collective-permute-start | bytes 1572872 | tf_op jit(solution)/shard_map/ppermute | solution.py:185
  116.7 15.1 %collective-permute-start.8 = (bf16[512,512]{1,0:T(8,128)(2,1)}, bf16[512,512]{1,0:T(8,128)(2,1)}, u32[]{:S(2)}, u32[]{:S(2)}) collective-permute-start(bf16[512,512]{1,0:T(8,128)(2,1)} %get-tuple-element.20), channel_id=1, source_target_pairs={{0,2},{1,3},{2,0},{3,1},{4,6},{5,7},{6,4},{7,5},{8,10},{9,11},{10,... | collective-permute-start | bytes 1572872 | tf_op jit(solution)/shard_map/ppermute | solution.py:185
  118.4 23.8 %collective-permute-start.9 = (bf16[512,512]{1,0:T(8,128)(2,1)}, bf16[512,512]{1,0:T(8,128)(2,1)}, u32[]{:S(2)}, u32[]{:S(2)}) collective-permute-start(bf16[512,512]{1,0:T(8,128)(2,1)} %get-tuple-element.19), channel_id=1, source_target_pairs={{0,3},{1,2},{2,1},{3,0},{4,7},{5,6},{6,5},{7,4},{8,11},{9,10},{10,... | collective-permute-start | bytes 1572872 | tf_op jit(solution)/shard_map/ppermute | solution.py:185
  118.6 24.6 %collective-permute-start.6 = (bf16[896,256]{1,0:T(8,128)(2,1)S(1)}, bf16[896,256]{1,0:T(8,128)(2,1)S(1)}, u32[]{:S(2)}, u32[]{:S(2)}) collective-permute-start(bf16[896,256]{1,0:T(8,128)(2,1)S(1)} %slice.65), channel_id=1, source_target_pairs={{0,4},{4,8},{8,12},{12,16},{16,20},{20,24},{24,28},{1,5},{5,9},{9,... | collective-permute-start | bytes 1376264 | tf_op jit(solution)/shard_map/ppermute | solution.py:138
  122.7 20.5 %copy-start.3 = (bf16[2048,256]{1,0:T(8,128)(2,1)S(1)}, bf16[2048,256]{1,0:T(8,128)(2,1)}, u32[]{:S(2)}) copy-start(bf16[2048,256]{1,0:T(8,128)(2,1)} %get-tuple-element.26) | copy-start | bytes 3145732
  158.5 6.9 %copy-start.11 = (bf16[512,512]{1,0:T(8,128)(2,1)S(1)}, bf16[512,512]{1,0:T(8,128)(2,1)}, u32[]{:S(2)}) copy-start(bf16[512,512]{1,0:T(8,128)(2,1)} %get-tuple-element.16) | copy-start | bytes 1572868
  158.5 8.6 %copy-start.10 = (bf16[512,512]{1,0:T(8,128)(2,1)S(1)}, bf16[512,512]{1,0:T(8,128)(2,1)}, u32[]{:S(2)}) copy-start(bf16[512,512]{1,0:T(8,128)(2,1)} %get-tuple-element.15) | copy-start | bytes 1572868
  158.5 55.4 %all-to-all-start.1 = ((bf16[16,128,512]{2,1,0:T(8,128)(2,1)}), bf16[16,128,512]{2,1,0:T(8,128)(2,1)S(1)}, u32[]{:S(2)}, u32[]{:S(2)}) async-start(bf16[16,128,512]{2,1,0:T(8,128)(2,1)} %attend.6), calls=%async_computation.1 | async-start | bytes 4194304 | tf_op jit(solution)/shard_map/all_to_all | solution.py:249
  165.4 2.1 collective-permute-start.10
  165.5 14.9 %collective-permute-start.11 = (bf16[512,512]{1,0:T(8,128)(2,1)S(1)}, bf16[512,512]{1,0:T(8,128)(2,1)S(1)}, u32[]{:S(2)}, u32[]{:S(2)}) collective-permute-start(bf16[512,512]{1,0:T(8,128)(2,1)S(1)} %copy-done.11), channel_id=1, source_target_pairs={{0,2},{1,3},{2,0},{3,1},{4,6},{5,7},{6,4},{7,5},{8,10},{9,11},{10,... | collective-permute-start | bytes 1572872 | tf_op jit(solution)/shard_map/ppermute | solution.py:185
  167.2 23.3 %collective-permute-start.12 = (bf16[512,512]{1,0:T(8,128)(2,1)S(1)}, bf16[512,512]{1,0:T(8,128)(2,1)S(1)}, u32[]{:S(2)}, u32[]{:S(2)}) collective-permute-start(bf16[512,512]{1,0:T(8,128)(2,1)S(1)} %copy-done.10), channel_id=1, source_target_pairs={{0,3},{1,2},{2,1},{3,0},{4,7},{5,6},{6,5},{7,4},{8,11},{9,10},{10,... | collective-permute-start | bytes 1572872 | tf_op jit(solution)/shard_map/ppermute | solution.py:185
  204.8 15.0 %copy-start.9 = (bf16[512,512]{1,0:T(8,128)(2,1)S(1)}, bf16[512,512]{1,0:T(8,128)(2,1)}, u32[]{:S(2)}) copy-start(bf16[512,512]{1,0:T(8,128)(2,1)} %get-tuple-element.23) | copy-start | bytes 1572868
  204.8 16.7 %copy-start.8 = (bf16[512,512]{1,0:T(8,128)(2,1)S(1)}, bf16[512,512]{1,0:T(8,128)(2,1)}, u32[]{:S(2)}) copy-start(bf16[512,512]{1,0:T(8,128)(2,1)} %get-tuple-element.22) | copy-start | bytes 1572868
  215.3 52.2 %all-to-all-start.3 = ((bf16[16,128,512]{2,1,0:T(8,128)(2,1)}), bf16[16,128,512]{2,1,0:T(8,128)(2,1)}, u32[]{:S(2)}, u32[]{:S(2)}) async-start(bf16[16,128,512]{2,1,0:T(8,128)(2,1)} %attend.7), calls=%async_computation.3 | async-start | bytes 4194304 | tf_op jit(solution)/shard_map/all_to_all | solution.py:249
  219.6 3.2 collective-permute-start
  219.7 15.0 %collective-permute-start.1 = (bf16[512,512]{1,0:T(8,128)(2,1)S(1)}, bf16[512,512]{1,0:T(8,128)(2,1)}, u32[]{:S(2)}, u32[]{:S(2)}) collective-permute-start(bf16[512,512]{1,0:T(8,128)(2,1)S(1)} %copy-done.9), channel_id=1, source_target_pairs={{0,2},{1,3},{2,0},{3,1},{4,6},{5,7},{6,4},{7,5},{8,10},{9,11},{10,... | collective-permute-start | bytes 1572872 | tf_op jit(solution)/shard_map/ppermute | solution.py:185
  221.4 23.4 %collective-permute-start.2 = (bf16[512,512]{1,0:T(8,128)(2,1)S(1)}, bf16[512,512]{1,0:T(8,128)(2,1)}, u32[]{:S(2)}, u32[]{:S(2)}) collective-permute-start(bf16[512,512]{1,0:T(8,128)(2,1)S(1)} %copy-done.8), channel_id=1, source_target_pairs={{0,3},{1,2},{2,1},{3,0},{4,7},{5,6},{6,5},{7,4},{8,11},{9,10},{10,... | collective-permute-start | bytes 1572872 | tf_op jit(solution)/shard_map/ppermute | solution.py:185
  267.5 52.0 %all-to-all-start = ((bf16[16,128,512]{2,1,0:T(8,128)(2,1)}), bf16[16,128,512]{2,1,0:T(8,128)(2,1)S(1)}, u32[]{:S(2)}, u32[]{:S(2)}) async-start(bf16[16,128,512]{2,1,0:T(8,128)(2,1)} %attend.5), calls=%async_computation | async-start | bytes 4194304 | tf_op jit(solution)/shard_map/all_to_all | solution.py:249
  (9 other events, 17.0 us)

commit v2 on v1

--- a/solution.py
+++ b/solution.py
@@ -12,12 +12,12 @@
 HD = 128
 BLK = 128
 MAXDOC = 8
-ROW_HEADS = 2
 
 
 def attend_kernel(heads, block_ref, count_ref, q_ref, kv_ref, o_ref):
     factor = math.log2(math.e) / math.sqrt(HD)
-    rows = ROW_HEADS * BLK
+    row_heads = max(1, heads // 2)
+    rows = row_heads * BLK
     row_pos = lax.rem(lax.broadcasted_iota(jnp.int32, (rows, BLK), 0), BLK)
     causal = lax.broadcasted_iota(jnp.int32, (rows, BLK), 1) <= row_pos
 
@@ -29,10 +29,10 @@
         values = kv_ref[pl.ds(first, width), HD:]
         inside = jnp.full((rows, BLK), count - (2 * pairs - 1), jnp.int32) > 0
         all_scores = []
-        for step in range(heads // ROW_HEADS):
-            base = step * ROW_HEADS * HD
+        for step in range(heads // row_heads):
+            base = step * row_heads * HD
             queries = jnp.concatenate(
-                [q_ref[q_rows, base + i * HD : base + (i + 1) * HD] for i in range(ROW_HEADS)],
+                [q_ref[q_rows, base + i * HD : base + (i + 1) * HD] for i in range(row_heads)],
                 axis=0,
             )
             all_scores.append(
@@ -40,8 +40,8 @@
                     queries, keys, (((1,), (1,)), ((), ())), preferred_element_type=jnp.float32
                 )
             )
-        for step in range(heads // ROW_HEADS):
-            base = step * ROW_HEADS * HD
+        for step in range(heads // row_heads):
+            base = step * row_heads * HD
             scores = all_scores[step]
             parts = [scores[:, i * BLK : (i + 1) * BLK] for i in range(2 * pairs)]
             parts[0] = jnp.where(inside, parts[0], -jnp.inf)
@@ -53,7 +53,7 @@
             weights = jnp.concatenate([part.astype(jnp.bfloat16) for part in parts], axis=1)
             mixed = jnp.dot(weights, values, preferred_element_type=jnp.float32) / total
             mixed = mixed.astype(o_ref.dtype)
-            for i in range(ROW_HEADS):
+            for i in range(row_heads):
                 o_ref[slot, :, base + i * HD : base + (i + 1) * HD] = mixed[
                     i * BLK : (i + 1) * BLK
                 ]

time: 325 us -> 325 us (level)
  no operation moved by 1% of the time
where the time goes in v2:
time: 325 us; the launch traced here: 323 us
  waiting for transfers between devices  149 us (46%)
  Pallas kernels  75.7 us (23%)
  starting transfers between devices  52.4 us (16%)
  local copies, waits for them, and re-layouts  34.7 us (11%)
  other arithmetic  11.3 us (3%)
    ppermute x12, waiting for transfers between devices, by_permutes(): lax.ppermute(piece, 'head', [(h, h ^ step) for h in range(head_count)])  76.9 us
    pallas_call x5, Pallas kernels, attend(): pl.pallas_call(functools.partial(attend_kernel, heads), out_shape=jax.Sha...  61.9 us
    all_to_all x5, waiting for transfers between devices, shards(): lax.all_to_all(out, 'ctx', split_axis=0, concat_axis=0, tiled=True)  53 us
    all_to_all x5, starting transfers between devices, shards(): lax.all_to_all(out, 'ctx', split_axis=0, concat_axis=0, tiled=True)  28.3 us
    dynamic_update_slice x14, local copies, waits for them, and re-layouts, by_permutes(): whole = lax.dynamic_update_slice(whole, piece, (other * local_rows, 0))  14.5 us
    pallas_call x5, Pallas kernels, place(): pl.pallas_call(functools.partial(place_kernel, first), out_shape=jax.Shap...  13.8 us
    all_to_all x2, waiting for transfers between devices, all_pairs(): lax.all_to_all(parts, 'head', split_axis=0, concat_axis=0, tiled=True)  11.3 us
    ppermute x2, starting transfers between devices, shifted(): return lax.ppermute(shard, axis, pairs)  8.81 us
  transfers between devices with their start and end apart: 21, of which 14 were waited for; matrix products, arithmetic and copies ran while one was open for 11% of the time, Pallas kernels for 19%

profile of v2, /device:TPU:0, one launch (start us, length us, event | category | flops | bytes accessed | tf_op | source)
XLA Modules:
  0.0 323.3 jit_solution(18323638030799028730)
XLA Ops:
  0.0 2.6 fusion.6
  3.9 4.3 %all-to-all-start.2 = ((bf16[4,512,256]{2,1,0:T(8,128)(2,1)}), bf16[4,512,256]{2,1,0:T(8,128)(2,1)S(1)}, u32[]{:S(2)}, u32[]{:S(2)}) async-start(bf16[4,512,256]{2,1,0:T(8,128)(2,1)} %pad_maximum_fusion.2), calls=%async_computation.2 | async-start | bytes 2097152 | tf_op jit(solution)/shard_map/all_to_all | solution.py:167
  11.3 11.3 %all-to-all-done.2 = bf16[4,512,256]{2,1,0:T(8,128)(2,1)S(1)} async-done(((bf16[4,512,256]{2,1,0:T(8,128)(2,1)}), bf16[4,512,256]{2,1,0:T(8,128)(2,1)S(1)}, u32[]{:S(2)}, u32[]{:S(2)}) %all-to-all-start.2) | async-done | bytes 1048608 | tf_op jit(solution)/shard_map/all_to_all | solution.py:167
  22.6 3.5 %all-to-all-start.5 = ((bf16[4,512,256]{2,1,0:T(8,128)(2,1)}), bf16[4,512,256]{2,1,0:T(8,128)(2,1)S(1)}, u32[]{:S(2)}, u32[]{:S(2)}) async-start(bf16[4,512,256]{2,1,0:T(8,128)(2,1)} %pad_maximum_fusion.3), calls=%async_computation.5 | async-start | bytes 2097152 | tf_op jit(solution)/shard_map/all_to_all | solution.py:167
  26.9 4.9 %collective-permute-start.13 = (bf16[896,256]{1,0:T(8,128)(2,1)}, bf16[896,256]{1,0:T(8,128)(2,1)}, u32[]{:S(2)}, u32[]{:S(2)}) collective-permute-start(bf16[896,256]{1,0:T(8,128)(2,1)} %slice.67), channel_id=1, source_target_pairs={{0,4},{4,8},{8,12},{12,16},{16,20},{20,24},{24,28},{1,5},{5,9},{9,... | collective-permute-start | bytes 1376264 | tf_op jit(solution)/shard_map/ppermute | solution.py:138
  34.3 7.4 %collective-permute-done.13 = bf16[896,256]{1,0:T(8,128)(2,1)} collective-permute-done((bf16[896,256]{1,0:T(8,128)(2,1)}, bf16[896,256]{1,0:T(8,128)(2,1)}, u32[]{:S(2)}, u32[]{:S(2)}) %collective-permute-start.13) | collective-permute-done | bytes 458784 | tf_op jit(solution)/shard_map/ppermute | solution.py:138
  44.9 10.7 %attend.9 = bf16[16,128,256]{2,1,0:T(8,128)(2,1)} custom-call(s32[16]{0:T(128)} %reduce_sum.40.block_ref, s32[16]{0:T(128)} %select_reduce_fusion.count_ref, bf16[2048,256]{1,0:T(8,128)(2,1)} %bitcast.24, bf16[2944,256]{1,0:T(8,128)(2,1)} %pad_maximum_fusion.1.kv_ref), custom_call_target="tpu_custom_call" | custom-call | flops 1342177280 | bytes 3604480 | tf_op jit(solution)/shard_map/attend/pallas_call | solution.py:80
  55.7 7.2 %all-to-all-start.6 = ((bf16[16,128,256]{2,1,0:T(8,128)(2,1)}), bf16[16,128,256]{2,1,0:T(8,128)(2,1)S(1)}, u32[]{:S(2)}, u32[]{:S(2)}) async-start(bf16[16,128,256]{2,1,0:T(8,128)(2,1)} %attend.9), calls=%async_computation.6 | async-start | bytes 2097152 | tf_op jit(solution)/shard_map/all_to_all | solution.py:249
  69.5 10.2 %collective-permute-done.4 = bf16[512,512]{1,0:T(8,128)(2,1)} collective-permute-done((bf16[512,512]{1,0:T(8,128)(2,1)}, bf16[512,512]{1,0:T(8,128)(2,1)}, u32[]{:S(2)}, u32[]{:S(2)}) %collective-permute-start.4) | collective-permute-done | bytes 524320 | tf_op jit(solution)/shard_map/ppermute | solution.py:185
  80.8 9.2 %collective-permute-done.5 = bf16[512,512]{1,0:T(8,128)(2,1)} collective-permute-done((bf16[512,512]{1,0:T(8,128)(2,1)}, bf16[512,512]{1,0:T(8,128)(2,1)}, u32[]{:S(2)}, u32[]{:S(2)}) %collective-permute-start.5) | collective-permute-done | bytes 524320 | tf_op jit(solution)/shard_map/ppermute | solution.py:185
  92.7 10.7 %attend.8 = bf16[16,128,256]{2,1,0:T(8,128)(2,1)} custom-call(s32[16]{0:T(128)} %reduce_sum.40.block_ref, s32[16]{0:T(128)} %select_reduce_fusion.count_ref, bf16[2048,256]{1,0:T(8,128)(2,1)} %get-tuple-element.25.q_ref, bf16[2944,256]{1,0:T(8,128)(2,1)} %pad_maximum_fusion.1.kv_ref), custom_call_target="tpu_custom_call" | custom-call | flops 1342177280 | bytes 3604480 | tf_op jit(solution)/shard_map/attend/pallas_call | solution.py:80
  103.4 6.3 %all-to-all-start.4 = ((bf16[16,128,256]{2,1,0:T(8,128)(2,1)}), bf16[16,128,256]{2,1,0:T(8,128)(2,1)}, u32[]{:S(2)}, u32[]{:S(2)}) async-start(bf16[16,128,256]{2,1,0:T(8,128)(2,1)} %attend.8), calls=%async_computation.4 | async-start | bytes 2097152 | tf_op jit(solution)/shard_map/all_to_all | solution.py:249
  109.8 4.8 %constant_dynamic-slice_fusion.5 = (bf16[512,512]{1,0:T(8,128)(2,1)}, bf16[512,512]{1,0:T(8,128)(2,1)}, bf16[512,512]{1,0:T(8,128)(2,1)}, bf16[2048,512]{1,0:T(8...) fusion(bf16[512,8192]{1,0:T(8,128)(2,1)} %param.5, ...), kind=kLoop, calls=%fused_computation.35 | loop fusion | bytes 10485804 | tf_op jit(solution)/shard_map/dynamic_slice | solution.py:174
  117.8 4.0 %collective-permute-start.6 = (bf16[896,256]{1,0:T(8,128)(2,1)S(1)}, bf16[896,256]{1,0:T(8,128)(2,1)S(1)}, u32[]{:S(2)}, u32[]{:S(2)}) collective-permute-start(bf16[896,256]{1,0:T(8,128)(2,1)S(1)} %slice.65), channel_id=1, source_target_pairs={{0,4},{4,8},{8,12},{12,16},{16,20},{20,24},{24,28},{1,5},{5,9},{9,... | collective-permute-start | bytes 1376264 | tf_op jit(solution)/shard_map/ppermute | solution.py:138
  124.2 6.8 %collective-permute-done.8 = bf16[512,512]{1,0:T(8,128)(2,1)} collective-permute-done((bf16[512,512]{1,0:T(8,128)(2,1)}, bf16[512,512]{1,0:T(8,128)(2,1)}, u32[]{:S(2)}, u32[]{:S(2)}) %collective-permute-start.8) | collective-permute-done | bytes 524320 | tf_op jit(solution)/shard_map/ppermute | solution.py:185
  132.1 9.2 %collective-permute-done.9 = bf16[512,512]{1,0:T(8,128)(2,1)} collective-permute-done((bf16[512,512]{1,0:T(8,128)(2,1)}, bf16[512,512]{1,0:T(8,128)(2,1)}, u32[]{:S(2)}, u32[]{:S(2)}) %collective-permute-start.9) | collective-permute-done | bytes 524320 | tf_op jit(solution)/shard_map/ppermute | solution.py:185
  144.2 13.5 %attend.6 = bf16[16,128,512]{2,1,0:T(8,128)(2,1)} custom-call(s32[16]{0:T(128)} %reduce_sum.40.block_ref, s32[16]{0:T(128)} %select_reduce_fusion.count_ref, bf16[2048,512]{1,0:T(8,128)(2,1)} %copy-done.6, bf16[2944,256]{1,0:T(8,128)(2,1)} %pad_maximum_fusion.kv_ref), custom_call_target="tpu_custom_call" | custom-call | flops 2684354560 | bytes 5701632 | tf_op jit(solution)/shard_map/attend/pallas_call | solution.py:80
  157.7 6.9 %all-to-all-start.1 = ((bf16[16,128,512]{2,1,0:T(8,128)(2,1)}), bf16[16,128,512]{2,1,0:T(8,128)(2,1)S(1)}, u32[]{:S(2)}, u32[]{:S(2)}) async-start(bf16[16,128,512]{2,1,0:T(8,128)(2,1)} %attend.6), calls=%async_computation.1 | async-start | bytes 4194304 | tf_op jit(solution)/shard_map/all_to_all | solution.py:249
  167.6 11.9 %collective-permute-done.11 = bf16[512,512]{1,0:T(8,128)(2,1)S(1)} collective-permute-done((bf16[512,512]{1,0:T(8,128)(2,1)S(1)}, bf16[512,512]{1,0:T(8,128)(2,1)S(1)}, u32[]{:S(2)}, u32[]{:S(2)}) %collective-permute-start.11) | collective-permute-done | bytes 524320 | tf_op jit(solution)/shard_map/ppermute | solution.py:185
  180.3 9.3 %collective-permute-done.12 = bf16[512,512]{1,0:T(8,128)(2,1)S(1)} collective-permute-done((bf16[512,512]{1,0:T(8,128)(2,1)S(1)}, bf16[512,512]{1,0:T(8,128)(2,1)S(1)}, u32[]{:S(2)}, u32[]{:S(2)}) %collective-permute-start.12) | collective-permute-done | bytes 524320 | tf_op jit(solution)/shard_map/ppermute | solution.py:185
  190.5 13.4 %attend.7 = bf16[16,128,512]{2,1,0:T(8,128)(2,1)} custom-call(s32[16]{0:T(128)} %reduce_sum.40.block_ref, s32[16]{0:T(128)} %select_reduce_fusion.count_ref, bf16[2048,512]{1,0:T(8,128)(2,1)} %constant_dynamic-update-slice_fusion.1.q_ref, bf16[2944,256]{1,0:T(8,128)(2,1)} %pad_maximum_fusion.1.kv_ref), custom_call_target="tpu_custom_call" | custom-call | flops 2684354560 | bytes 5701632 | tf_op jit(solution)/shard_map/attend/pallas_call | solution.py:80
  204.0 9.2 %all-to-all-done.1.x_ref = bf16[16,128,512]{2,1,0:T(8,128)(2,1)S(1)} async-done(((bf16[16,128,512]{2,1,0:T(8,128)(2,1)}), bf16[16,128,512]{2,1,0:T(8,128)(2,1)S(1)}, u32[]{:S(2)}, u32[]{:S(2)}) %all-to-all-start.1) | async-done | bytes 2097184 | tf_op jit(solution)/shard_map/all_to_all | solution.py:249
  214.5 4.4 %all-to-all-start.3 = ((bf16[16,128,512]{2,1,0:T(8,128)(2,1)}), bf16[16,128,512]{2,1,0:T(8,128)(2,1)}, u32[]{:S(2)}, u32[]{:S(2)}) async-start(bf16[16,128,512]{2,1,0:T(8,128)(2,1)} %attend.7), calls=%async_computation.3 | async-start | bytes 4194304 | tf_op jit(solution)/shard_map/all_to_all | solution.py:249
  223.1 10.8 %collective-permute-done.1 = bf16[512,512]{1,0:T(8,128)(2,1)} collective-permute-done((bf16[512,512]{1,0:T(8,128)(2,1)S(1)}, bf16[512,512]{1,0:T(8,128)(2,1)}, u32[]{:S(2)}, u32[]{:S(2)}) %collective-permute-start.1) | collective-permute-done | bytes 524320 | tf_op jit(solution)/shard_map/ppermute | solution.py:185
  235.0 9.1 %collective-permute-done.2 = bf16[512,512]{1,0:T(8,128)(2,1)} collective-permute-done((bf16[512,512]{1,0:T(8,128)(2,1)S(1)}, bf16[512,512]{1,0:T(8,128)(2,1)}, u32[]{:S(2)}, u32[]{:S(2)}) %collective-permute-start.2) | collective-permute-done | bytes 524320 | tf_op jit(solution)/shard_map/ppermute | solution.py:185
  246.4 13.5 %attend.5 = bf16[16,128,512]{2,1,0:T(8,128)(2,1)} custom-call(s32[16]{0:T(128)} %reduce_sum.40.block_ref, s32[16]{0:T(128)} %select_reduce_fusion.count_ref, bf16[2048,512]{1,0:T(8,128)(2,1)} %copy-done.5, bf16[2944,256]{1,0:T(8,128)(2,1)} %pad_maximum_fusion.kv_ref), custom_call_target="tpu_custom_call" | custom-call | flops 2684354560 | bytes 5701632 | tf_op jit(solution)/shard_map/attend/pallas_call | solution.py:80
  260.0 6.7 %all-to-all-done.3.x_ref = bf16[16,128,512]{2,1,0:T(8,128)(2,1)} async-done(((bf16[16,128,512]{2,1,0:T(8,128)(2,1)}), bf16[16,128,512]{2,1,0:T(8,128)(2,1)}, u32[]{:S(2)}, u32[]{:S(2)}) %all-to-all-start.3) | async-done | bytes 2097184 | tf_op jit(solution)/shard_map/all_to_all | solution.py:249
  266.7 3.6 %all-to-all-start = ((bf16[16,128,512]{2,1,0:T(8,128)(2,1)}), bf16[16,128,512]{2,1,0:T(8,128)(2,1)S(1)}, u32[]{:S(2)}, u32[]{:S(2)}) async-start(bf16[16,128,512]{2,1,0:T(8,128)(2,1)} %attend.5), calls=%async_computation | async-start | bytes 4194304 | tf_op jit(solution)/shard_map/all_to_all | solution.py:249
  275.4 3.0 place.7.rest_0_
  278.5 3.0 place.8.rest_0_
  281.6 37.1 %all-to-all-done.x_ref = bf16[16,128,512]{2,1,0:T(8,128)(2,1)S(1)} async-done(((bf16[16,128,512]{2,1,0:T(8,128)(2,1)}), bf16[16,128,512]{2,1,0:T(8,128)(2,1)S(1)}, u32[]{:S(2)}, u32[]{:S(2)}) %all-to-all-start) | async-done | bytes 2097184 | tf_op jit(solution)/shard_map/all_to_all | solution.py:249
  320.1 3.0 place.9
  (116 shorter events, 51.0 us)
Async XLA Ops:
  3.9 18.7 %all-to-all-start.2 = ((bf16[4,512,256]{2,1,0:T(8,128)(2,1)}), bf16[4,512,256]{2,1,0:T(8,128)(2,1)S(1)}, u32[]{:S(2)}, u32[]{:S(2)}) async-start(bf16[4,512,256]{2,1,0:T(8,128)(2,1)} %pad_maximum_fusion.2), calls=%async_computation.2 | async-start | bytes 2097152 | tf_op jit(solution)/shard_map/all_to_all | solution.py:167
  22.6 21.4 %all-to-all-start.5 = ((bf16[4,512,256]{2,1,0:T(8,128)(2,1)}), bf16[4,512,256]{2,1,0:T(8,128)(2,1)S(1)}, u32[]{:S(2)}, u32[]{:S(2)}) async-start(bf16[4,512,256]{2,1,0:T(8,128)(2,1)} %pad_maximum_fusion.3), calls=%async_computation.5 | async-start | bytes 2097152 | tf_op jit(solution)/shard_map/all_to_all | solution.py:167
  26.9 14.8 %collective-permute-start.13 = (bf16[896,256]{1,0:T(8,128)(2,1)}, bf16[896,256]{1,0:T(8,128)(2,1)}, u32[]{:S(2)}, u32[]{:S(2)}) collective-permute-start(bf16[896,256]{1,0:T(8,128)(2,1)} %slice.67), channel_id=1, source_target_pairs={{0,4},{4,8},{8,12},{12,16},{16,20},{20,24},{24,28},{1,5},{5,9},{9,... | collective-permute-start | bytes 1376264 | tf_op jit(solution)/shard_map/ppermute | solution.py:138
  55.7 7.2 %copy-start.16 = (bf16[512,128]{1,0:T(8,128)(2,1)S(1)}, bf16[512,128]{1,0:T(8,128)(2,1)}, u32[]{:S(2)}) copy-start(bf16[512,128]{1,0:T(8,128)(2,1)} %get-tuple-element.31) | copy-start | bytes 393220
  55.7 7.2 %copy-start.17 = (bf16[512,128]{1,0:T(8,128)(2,1)S(1)}, bf16[512,128]{1,0:T(8,128)(2,1)}, u32[]{:S(2)}) copy-start(bf16[512,128]{1,0:T(8,128)(2,1)} %get-tuple-element.46) | copy-start | bytes 393220
  55.7 8.1 %copy-start.14 = (bf16[512,128]{1,0:T(8,128)(2,1)S(1)}, bf16[512,128]{1,0:T(8,128)(2,1)}, u32[]{:S(2)}) copy-start(bf16[512,128]{1,0:T(8,128)(2,1)} %get-tuple-element.30) | copy-start | bytes 393220
  55.7 8.1 %copy-start.15 = (bf16[512,128]{1,0:T(8,128)(2,1)S(1)}, bf16[512,128]{1,0:T(8,128)(2,1)}, u32[]{:S(2)}) copy-start(bf16[512,128]{1,0:T(8,128)(2,1)} %get-tuple-element.47) | copy-start | bytes 393220
  55.7 10.6 %copy-start.12 = (bf16[512,128]{1,0:T(8,128)(2,1)S(1)}, bf16[512,128]{1,0:T(8,128)(2,1)}, u32[]{:S(2)}) copy-start(bf16[512,128]{1,0:T(8,128)(2,1)} %get-tuple-element.29) | copy-start | bytes 393220
  55.7 10.6 %copy-start.13 = (bf16[512,128]{1,0:T(8,128)(2,1)S(1)}, bf16[512,128]{1,0:T(8,128)(2,1)}, u32[]{:S(2)}) copy-start(bf16[512,128]{1,0:T(8,128)(2,1)} %get-tuple-element.48) | copy-start | bytes 393220
  55.7 47.7 %all-to-all-start.6 = ((bf16[16,128,256]{2,1,0:T(8,128)(2,1)}), bf16[16,128,256]{2,1,0:T(8,128)(2,1)S(1)}, u32[]{:S(2)}, u32[]{:S(2)}) async-start(bf16[16,128,256]{2,1,0:T(8,128)(2,1)} %attend.9), calls=%async_computation.6 | async-start | bytes 2097152 | tf_op jit(solution)/shard_map/all_to_all | solution.py:249
  63.8 4.7 %collective-permute-start.3 = (bf16[512,512]{1,0:T(8,128)(2,1)}, bf16[512,512]{1,0:T(8,128)(2,1)}, u32[]{:S(2)}, u32[]{:S(2)}) collective-permute-start(bf16[512,512]{1,0:T(8,128)(2,1)} %pad_maximum_fusion.4), channel_id=1, source_target_pairs={{0,1},{1,0},{2,3},{3,2},{4,5},{5,4},{6,7},{7,6},{8,9},{9,8},{10,11... | collective-permute-start | bytes 1572872 | tf_op jit(solution)/shard_map/ppermute | solution.py:185
  64.6 15.1 %collective-permute-start.4 = (bf16[512,512]{1,0:T(8,128)(2,1)}, bf16[512,512]{1,0:T(8,128)(2,1)}, u32[]{:S(2)}, u32[]{:S(2)}) collective-permute-start(bf16[512,512]{1,0:T(8,128)(2,1)} %pad_maximum_fusion.5), channel_id=1, source_target_pairs={{0,2},{1,3},{2,0},{3,1},{4,6},{5,7},{6,4},{7,5},{8,10},{9,11},{10,... | collective-permute-start | bytes 1572872 | tf_op jit(solution)/shard_map/ppermute | solution.py:185
  67.1 22.9 %collective-permute-start.5 = (bf16[512,512]{1,0:T(8,128)(2,1)}, bf16[512,512]{1,0:T(8,128)(2,1)}, u32[]{:S(2)}, u32[]{:S(2)}) collective-permute-start(bf16[512,512]{1,0:T(8,128)(2,1)} %pad_maximum_fusion.6), channel_id=1, source_target_pairs={{0,3},{1,2},{2,1},{3,0},{4,7},{5,6},{6,5},{7,4},{8,11},{9,10},{10,... | collective-permute-start | bytes 1572872 | tf_op jit(solution)/shard_map/ppermute | solution.py:185
  103.4 54.3 %all-to-all-start.4 = ((bf16[16,128,256]{2,1,0:T(8,128)(2,1)}), bf16[16,128,256]{2,1,0:T(8,128)(2,1)}, u32[]{:S(2)}, u32[]{:S(2)}) async-start(bf16[16,128,256]{2,1,0:T(8,128)(2,1)} %attend.8), calls=%async_computation.4 | async-start | bytes 2097152 | tf_op jit(solution)/shard_map/all_to_all | solution.py:249
  115.9 7.2 %collective-permute-start.7 = (bf16[512,512]{1,0:T(8,128)(2,1)}, bf16[512,512]{1,0:T(8,128)(2,1)}, u32[]{:S(2)}, u32[]{:S(2)}) collective-permute-start(bf16[512,512]{1,0:T(8,128)(2,1)} %get-tuple-element.21), channel_id=1, source_target_pairs={{0,1},{1,0},{2,3},{3,2},{4,5},{5,4},{6,7},{7,6},{8,9},{9,8},{10,11... | collective-permute-start | bytes 1572872 | tf_op jit(solution)/shard_map/ppermute | solution.py:185
  115.9 15.1 %collective-permute-start.8 = (bf16[512,512]{1,0:T(8,128)(2,1)}, bf16[512,512]{1,0:T(8,128)(2,1)}, u32[]{:S(2)}, u32[]{:S(2)}) collective-permute-start(bf16[512,512]{1,0:T(8,128)(2,1)} %get-tuple-element.20), channel_id=1, source_target_pairs={{0,2},{1,3},{2,0},{3,1},{4,6},{5,7},{6,4},{7,5},{8,10},{9,11},{10,... | collective-permute-start | bytes 1572872 | tf_op jit(solution)/shard_map/ppermute | solution.py:185
  117.6 23.8 %collective-permute-start.9 = (bf16[512,512]{1,0:T(8,128)(2,1)}, bf16[512,512]{1,0:T(8,128)(2,1)}, u32[]{:S(2)}, u32[]{:S(2)}) collective-permute-start(bf16[512,512]{1,0:T(8,128)(2,1)} %get-tuple-element.19), channel_id=1, source_target_pairs={{0,3},{1,2},{2,1},{3,0},{4,7},{5,6},{6,5},{7,4},{8,11},{9,10},{10,... | collective-permute-start | bytes 1572872 | tf_op jit(solution)/shard_map/ppermute | solution.py:185
  117.8 24.6 %collective-permute-start.6 = (bf16[896,256]{1,0:T(8,128)(2,1)S(1)}, bf16[896,256]{1,0:T(8,128)(2,1)S(1)}, u32[]{:S(2)}, u32[]{:S(2)}) collective-permute-start(bf16[896,256]{1,0:T(8,128)(2,1)S(1)} %slice.65), channel_id=1, source_target_pairs={{0,4},{4,8},{8,12},{12,16},{16,20},{20,24},{24,28},{1,5},{5,9},{9,... | collective-permute-start | bytes 1376264 | tf_op jit(solution)/shard_map/ppermute | solution.py:138
  121.9 20.5 %copy-start.3 = (bf16[2048,256]{1,0:T(8,128)(2,1)S(1)}, bf16[2048,256]{1,0:T(8,128)(2,1)}, u32[]{:S(2)}) copy-start(bf16[2048,256]{1,0:T(8,128)(2,1)} %get-tuple-element.26) | copy-start | bytes 3145732
  157.7 6.9 %copy-start.11 = (bf16[512,512]{1,0:T(8,128)(2,1)S(1)}, bf16[512,512]{1,0:T(8,128)(2,1)}, u32[]{:S(2)}) copy-start(bf16[512,512]{1,0:T(8,128)(2,1)} %get-tuple-element.16) | copy-start | bytes 1572868
  157.7 8.6 %copy-start.10 = (bf16[512,512]{1,0:T(8,128)(2,1)S(1)}, bf16[512,512]{1,0:T(8,128)(2,1)}, u32[]{:S(2)}) copy-start(bf16[512,512]{1,0:T(8,128)(2,1)} %get-tuple-element.15) | copy-start | bytes 1572868
  157.7 55.4 %all-to-all-start.1 = ((bf16[16,128,512]{2,1,0:T(8,128)(2,1)}), bf16[16,128,512]{2,1,0:T(8,128)(2,1)S(1)}, u32[]{:S(2)}, u32[]{:S(2)}) async-start(bf16[16,128,512]{2,1,0:T(8,128)(2,1)} %attend.6), calls=%async_computation.1 | async-start | bytes 4194304 | tf_op jit(solution)/shard_map/all_to_all | solution.py:249
  164.6 2.1 collective-permute-start.10
  164.7 14.9 %collective-permute-start.11 = (bf16[512,512]{1,0:T(8,128)(2,1)S(1)}, bf16[512,512]{1,0:T(8,128)(2,1)S(1)}, u32[]{:S(2)}, u32[]{:S(2)}) collective-permute-start(bf16[512,512]{1,0:T(8,128)(2,1)S(1)} %copy-done.11), channel_id=1, source_target_pairs={{0,2},{1,3},{2,0},{3,1},{4,6},{5,7},{6,4},{7,5},{8,10},{9,11},{10,... | collective-permute-start | bytes 1572872 | tf_op jit(solution)/shard_map/ppermute | solution.py:185
  166.4 23.3 %collective-permute-start.12 = (bf16[512,512]{1,0:T(8,128)(2,1)S(1)}, bf16[512,512]{1,0:T(8,128)(2,1)S(1)}, u32[]{:S(2)}, u32[]{:S(2)}) collective-permute-start(bf16[512,512]{1,0:T(8,128)(2,1)S(1)} %copy-done.10), channel_id=1, source_target_pairs={{0,3},{1,2},{2,1},{3,0},{4,7},{5,6},{6,5},{7,4},{8,11},{9,10},{10,... | collective-permute-start | bytes 1572872 | tf_op jit(solution)/shard_map/ppermute | solution.py:185
  204.0 15.0 %copy-start.9 = (bf16[512,512]{1,0:T(8,128)(2,1)S(1)}, bf16[512,512]{1,0:T(8,128)(2,1)}, u32[]{:S(2)}) copy-start(bf16[512,512]{1,0:T(8,128)(2,1)} %get-tuple-element.23) | copy-start | bytes 1572868
  204.0 16.7 %copy-start.8 = (bf16[512,512]{1,0:T(8,128)(2,1)S(1)}, bf16[512,512]{1,0:T(8,128)(2,1)}, u32[]{:S(2)}) copy-start(bf16[512,512]{1,0:T(8,128)(2,1)} %get-tuple-element.22) | copy-start | bytes 1572868
  214.5 52.2 %all-to-all-start.3 = ((bf16[16,128,512]{2,1,0:T(8,128)(2,1)}), bf16[16,128,512]{2,1,0:T(8,128)(2,1)}, u32[]{:S(2)}, u32[]{:S(2)}) async-start(bf16[16,128,512]{2,1,0:T(8,128)(2,1)} %attend.7), calls=%async_computation.3 | async-start | bytes 4194304 | tf_op jit(solution)/shard_map/all_to_all | solution.py:249
  218.8 3.2 collective-permute-start
  218.9 15.0 %collective-permute-start.1 = (bf16[512,512]{1,0:T(8,128)(2,1)S(1)}, bf16[512,512]{1,0:T(8,128)(2,1)}, u32[]{:S(2)}, u32[]{:S(2)}) collective-permute-start(bf16[512,512]{1,0:T(8,128)(2,1)S(1)} %copy-done.9), channel_id=1, source_target_pairs={{0,2},{1,3},{2,0},{3,1},{4,6},{5,7},{6,4},{7,5},{8,10},{9,11},{10,... | collective-permute-start | bytes 1572872 | tf_op jit(solution)/shard_map/ppermute | solution.py:185
  220.6 23.4 %collective-permute-start.2 = (bf16[512,512]{1,0:T(8,128)(2,1)S(1)}, bf16[512,512]{1,0:T(8,128)(2,1)}, u32[]{:S(2)}, u32[]{:S(2)}) collective-permute-start(bf16[512,512]{1,0:T(8,128)(2,1)S(1)} %copy-done.8), channel_id=1, source_target_pairs={{0,3},{1,2},{2,1},{3,0},{4,7},{5,6},{6,5},{7,4},{8,11},{9,10},{10,... | collective-permute-start | bytes 1572872 | tf_op jit(solution)/shard_map/ppermute | solution.py:185
  266.7 52.0 %all-to-all-start = ((bf16[16,128,512]{2,1,0:T(8,128)(2,1)}), bf16[16,128,512]{2,1,0:T(8,128)(2,1)S(1)}, u32[]{:S(2)}, u32[]{:S(2)}) async-start(bf16[16,128,512]{2,1,0:T(8,128)(2,1)} %attend.5), calls=%async_computation | async-start | bytes 4194304 | tf_op jit(solution)/shard_map/all_to_all | solution.py:249
  (9 other events, 16.9 us)

commit v3 on v2

--- a/solution.py
+++ b/solution.py
@@ -14,7 +14,7 @@
 MAXDOC = 8
 
 
-def attend_kernel(heads, block_ref, count_ref, q_ref, kv_ref, o_ref):
+def attend_kernel(heads, block_ref, count_ref, q_ref, kv_ref, o_ref, turned_ref):
     factor = math.log2(math.e) / math.sqrt(HD)
     row_heads = max(1, heads // 2)
     rows = row_heads * BLK
@@ -25,7 +25,7 @@
         width = 2 * pairs * BLK
         first = pl.multiple_of((block + MAXDOC - 2 * pairs) * BLK, BLK)
         q_rows = pl.ds(pl.multiple_of(block * BLK, BLK), BLK)
-        keys = kv_ref[pl.ds(first, width), :HD]
+        keys = turned_ref[:, pl.ds(first, width)]
         values = kv_ref[pl.ds(first, width), HD:]
         inside = jnp.full((rows, BLK), count - (2 * pairs - 1), jnp.int32) > 0
         all_scores = []
@@ -37,7 +37,7 @@
             )
             all_scores.append(
                 lax.dot_general(
-                    queries, keys, (((1,), (1,)), ((), ())), preferred_element_type=jnp.float32
+                    queries, keys, (((1,), (0,)), ((), ())), preferred_element_type=jnp.float32
                 )
             )
         for step in range(heads // row_heads):
@@ -69,6 +69,8 @@
 
         return carry
 
+    for i in range(kv_ref.shape[0] // BLK):
+        turned_ref[:, i * BLK : (i + 1) * BLK] = kv_ref[i * BLK : (i + 1) * BLK, :HD].T
     lax.fori_loop(0, o_ref.shape[0], one, 0)
 
 
@@ -83,6 +85,7 @@
         in_specs=[pl.BlockSpec(memory_space=pltpu.SMEM)] * 2
         + [pl.BlockSpec(memory_space=pltpu.VMEM)] * 2,
         out_specs=pl.BlockSpec(memory_space=pltpu.VMEM),
+        scratch_shapes=[pltpu.VMEM((HD, window.shape[0]), jnp.bfloat16)],
         cost_estimate=pl.CostEstimate(
             flops=flops, transcendentals=0, bytes_accessed=4 * queries.size + 2 * window.size
         ),

time: 325 us -> 325 us (level)
  no operation moved by 1% of the time
where the time goes in v3:
time: 325 us; the launch traced here: 323 us
  waiting for transfers between devices  149 us (46%)
  Pallas kernels  75.6 us (23%)
  starting transfers between devices  52.4 us (16%)
  local copies, waits for them, and re-layouts  34.7 us (11%)
  other arithmetic  11.3 us (3%)
    ppermute x12, waiting for transfers between devices, by_permutes(): lax.ppermute(piece, 'head', [(h, h ^ step) for h in range(head_count)])  76.9 us
    pallas_call x5, Pallas kernels, attend(): pl.pallas_call(functools.partial(attend_kernel, heads), out_shape=jax.Sha...  61.8 us
    all_to_all x5, waiting for transfers between devices, shards(): lax.all_to_all(out, 'ctx', split_axis=0, concat_axis=0, tiled=True)  53.1 us
    all_to_all x5, starting transfers between devices, shards(): lax.all_to_all(out, 'ctx', split_axis=0, concat_axis=0, tiled=True)  28.3 us
    dynamic_update_slice x14, local copies, waits for them, and re-layouts, by_permutes(): whole = lax.dynamic_update_slice(whole, piece, (other * local_rows, 0))  14.5 us
    pallas_call x5, Pallas kernels, place(): pl.pallas_call(functools.partial(place_kernel, first), out_shape=jax.Shap...  13.8 us
    all_to_all x2, waiting for transfers between devices, all_pairs(): lax.all_to_all(parts, 'head', split_axis=0, concat_axis=0, tiled=True)  11.3 us
    ppermute x2, starting transfers between devices, shifted(): return lax.ppermute(shard, axis, pairs)  8.81 us
  transfers between devices with their start and end apart: 21, of which 14 were waited for; matrix products, arithmetic and copies ran while one was open for 11% of the time, Pallas kernels for 19%

profile of v3, /device:TPU:0, one launch (start us, length us, event | category | flops | bytes accessed | tf_op | source)
XLA Modules:
  0.0 323.2 jit_solution(4979299541451367761)
XLA Ops:
  0.0 2.6 fusion.6
  3.9 4.3 %all-to-all-start.2 = ((bf16[4,512,256]{2,1,0:T(8,128)(2,1)}), bf16[4,512,256]{2,1,0:T(8,128)(2,1)S(1)}, u32[]{:S(2)}, u32[]{:S(2)}) async-start(bf16[4,512,256]{2,1,0:T(8,128)(2,1)} %pad_maximum_fusion.2), calls=%async_computation.2 | async-start | bytes 2097152 | tf_op jit(solution)/shard_map/all_to_all | solution.py:170
  11.3 11.3 %all-to-all-done.2 = bf16[4,512,256]{2,1,0:T(8,128)(2,1)S(1)} async-done(((bf16[4,512,256]{2,1,0:T(8,128)(2,1)}), bf16[4,512,256]{2,1,0:T(8,128)(2,1)S(1)}, u32[]{:S(2)}, u32[]{:S(2)}) %all-to-all-start.2) | async-done | bytes 1048608 | tf_op jit(solution)/shard_map/all_to_all | solution.py:170
  22.6 3.5 %all-to-all-start.5 = ((bf16[4,512,256]{2,1,0:T(8,128)(2,1)}), bf16[4,512,256]{2,1,0:T(8,128)(2,1)S(1)}, u32[]{:S(2)}, u32[]{:S(2)}) async-start(bf16[4,512,256]{2,1,0:T(8,128)(2,1)} %pad_maximum_fusion.3), calls=%async_computation.5 | async-start | bytes 2097152 | tf_op jit(solution)/shard_map/all_to_all | solution.py:170
  26.9 4.9 %collective-permute-start.13 = (bf16[896,256]{1,0:T(8,128)(2,1)}, bf16[896,256]{1,0:T(8,128)(2,1)}, u32[]{:S(2)}, u32[]{:S(2)}) collective-permute-start(bf16[896,256]{1,0:T(8,128)(2,1)} %slice.67), channel_id=1, source_target_pairs={{0,4},{4,8},{8,12},{12,16},{16,20},{20,24},{24,28},{1,5},{5,9},{9,... | collective-permute-start | bytes 1376264 | tf_op jit(solution)/shard_map/ppermute | solution.py:141
  34.3 7.4 %collective-permute-done.13 = bf16[896,256]{1,0:T(8,128)(2,1)} collective-permute-done((bf16[896,256]{1,0:T(8,128)(2,1)}, bf16[896,256]{1,0:T(8,128)(2,1)}, u32[]{:S(2)}, u32[]{:S(2)}) %collective-permute-start.13) | collective-permute-done | bytes 458784 | tf_op jit(solution)/shard_map/ppermute | solution.py:141
  44.9 10.7 %attend.9 = bf16[16,128,256]{2,1,0:T(8,128)(2,1)} custom-call(s32[16]{0:T(128)} %reduce_sum.40.block_ref, s32[16]{0:T(128)} %select_reduce_fusion.count_ref, bf16[2048,256]{1,0:T(8,128)(2,1)} %bitcast.24, bf16[2944,256]{1,0:T(8,128)(2,1)} %pad_maximum_fusion.1.kv_ref), custom_call_target="tpu_custom_call" | custom-call | flops 1342177280 | bytes 3604480 | tf_op jit(solution)/shard_map/attend/pallas_call | solution.py:82
  55.7 7.2 %all-to-all-start.6 = ((bf16[16,128,256]{2,1,0:T(8,128)(2,1)}), bf16[16,128,256]{2,1,0:T(8,128)(2,1)S(1)}, u32[]{:S(2)}, u32[]{:S(2)}) async-start(bf16[16,128,256]{2,1,0:T(8,128)(2,1)} %attend.9), calls=%async_computation.6 | async-start | bytes 2097152 | tf_op jit(solution)/shard_map/all_to_all | solution.py:252
  69.5 10.2 %collective-permute-done.4 = bf16[512,512]{1,0:T(8,128)(2,1)} collective-permute-done((bf16[512,512]{1,0:T(8,128)(2,1)}, bf16[512,512]{1,0:T(8,128)(2,1)}, u32[]{:S(2)}, u32[]{:S(2)}) %collective-permute-start.4) | collective-permute-done | bytes 524320 | tf_op jit(solution)/shard_map/ppermute | solution.py:188
  80.8 9.2 %collective-permute-done.5 = bf16[512,512]{1,0:T(8,128)(2,1)} collective-permute-done((bf16[512,512]{1,0:T(8,128)(2,1)}, bf16[512,512]{1,0:T(8,128)(2,1)}, u32[]{:S(2)}, u32[]{:S(2)}) %collective-permute-start.5) | collective-permute-done | bytes 524320 | tf_op jit(solution)/shard_map/ppermute | solution.py:188
  92.7 10.7 %attend.8 = bf16[16,128,256]{2,1,0:T(8,128)(2,1)} custom-call(s32[16]{0:T(128)} %reduce_sum.40.block_ref, s32[16]{0:T(128)} %select_reduce_fusion.count_ref, bf16[2048,256]{1,0:T(8,128)(2,1)} %get-tuple-element.25.q_ref, bf16[2944,256]{1,0:T(8,128)(2,1)} %pad_maximum_fusion.1.kv_ref), custom_call_target="tpu_custom_call" | custom-call | flops 1342177280 | bytes 3604480 | tf_op jit(solution)/shard_map/attend/pallas_call | solution.py:82
  103.4 6.2 %all-to-all-start.4 = ((bf16[16,128,256]{2,1,0:T(8,128)(2,1)}), bf16[16,128,256]{2,1,0:T(8,128)(2,1)}, u32[]{:S(2)}, u32[]{:S(2)}) async-start(bf16[16,128,256]{2,1,0:T(8,128)(2,1)} %attend.8), calls=%async_computation.4 | async-start | bytes 2097152 | tf_op jit(solution)/shard_map/all_to_all | solution.py:252
  109.8 4.8 %constant_dynamic-slice_fusion.5 = (bf16[512,512]{1,0:T(8,128)(2,1)}, bf16[512,512]{1,0:T(8,128)(2,1)}, bf16[512,512]{1,0:T(8,128)(2,1)}, bf16[2048,512]{1,0:T(8...) fusion(bf16[512,8192]{1,0:T(8,128)(2,1)} %param.5, ...), kind=kLoop, calls=%fused_computation.35 | loop fusion | bytes 10485804 | tf_op jit(solution)/shard_map/dynamic_slice | solution.py:177
  117.8 4.0 %collective-permute-start.6 = (bf16[896,256]{1,0:T(8,128)(2,1)S(1)}, bf16[896,256]{1,0:T(8,128)(2,1)S(1)}, u32[]{:S(2)}, u32[]{:S(2)}) collective-permute-start(bf16[896,256]{1,0:T(8,128)(2,1)S(1)} %slice.65), channel_id=1, source_target_pairs={{0,4},{4,8},{8,12},{12,16},{16,20},{20,24},{24,28},{1,5},{5,9},{9,... | collective-permute-start | bytes 1376264 | tf_op jit(solution)/shard_map/ppermute | solution.py:141
  124.2 6.8 %collective-permute-done.8 = bf16[512,512]{1,0:T(8,128)(2,1)} collective-permute-done((bf16[512,512]{1,0:T(8,128)(2,1)}, bf16[512,512]{1,0:T(8,128)(2,1)}, u32[]{:S(2)}, u32[]{:S(2)}) %collective-permute-start.8) | collective-permute-done | bytes 524320 | tf_op jit(solution)/shard_map/ppermute | solution.py:188
  132.1 9.2 %collective-permute-done.9 = bf16[512,512]{1,0:T(8,128)(2,1)} collective-permute-done((bf16[512,512]{1,0:T(8,128)(2,1)}, bf16[512,512]{1,0:T(8,128)(2,1)}, u32[]{:S(2)}, u32[]{:S(2)}) %collective-permute-start.9) | collective-permute-done | bytes 524320 | tf_op jit(solution)/shard_map/ppermute | solution.py:188
  144.2 13.5 %attend.6 = bf16[16,128,512]{2,1,0:T(8,128)(2,1)} custom-call(s32[16]{0:T(128)} %reduce_sum.40.block_ref, s32[16]{0:T(128)} %select_reduce_fusion.count_ref, bf16[2048,512]{1,0:T(8,128)(2,1)} %copy-done.6, bf16[2944,256]{1,0:T(8,128)(2,1)} %pad_maximum_fusion.kv_ref), custom_call_target="tpu_custom_call" | custom-call | flops 2684354560 | bytes 5701632 | tf_op jit(solution)/shard_map/attend/pallas_call | solution.py:82
  157.7 6.9 %all-to-all-start.1 = ((bf16[16,128,512]{2,1,0:T(8,128)(2,1)}), bf16[16,128,512]{2,1,0:T(8,128)(2,1)S(1)}, u32[]{:S(2)}, u32[]{:S(2)}) async-start(bf16[16,128,512]{2,1,0:T(8,128)(2,1)} %attend.6), calls=%async_computation.1 | async-start | bytes 4194304 | tf_op jit(solution)/shard_map/all_to_all | solution.py:252
  167.6 11.9 %collective-permute-done.11 = bf16[512,512]{1,0:T(8,128)(2,1)S(1)} collective-permute-done((bf16[512,512]{1,0:T(8,128)(2,1)S(1)}, bf16[512,512]{1,0:T(8,128)(2,1)S(1)}, u32[]{:S(2)}, u32[]{:S(2)}) %collective-permute-start.11) | collective-permute-done | bytes 524320 | tf_op jit(solution)/shard_map/ppermute | solution.py:188
  180.3 9.3 %collective-permute-done.12 = bf16[512,512]{1,0:T(8,128)(2,1)S(1)} collective-permute-done((bf16[512,512]{1,0:T(8,128)(2,1)S(1)}, bf16[512,512]{1,0:T(8,128)(2,1)S(1)}, u32[]{:S(2)}, u32[]{:S(2)}) %collective-permute-start.12) | collective-permute-done | bytes 524320 | tf_op jit(solution)/shard_map/ppermute | solution.py:188
  190.5 13.4 %attend.7 = bf16[16,128,512]{2,1,0:T(8,128)(2,1)} custom-call(s32[16]{0:T(128)} %reduce_sum.40.block_ref, s32[16]{0:T(128)} %select_reduce_fusion.count_ref, bf16[2048,512]{1,0:T(8,128)(2,1)} %constant_dynamic-update-slice_fusion.1.q_ref, bf16[2944,256]{1,0:T(8,128)(2,1)} %pad_maximum_fusion.1.kv_ref), custom_call_target="tpu_custom_call" | custom-call | flops 2684354560 | bytes 5701632 | tf_op jit(solution)/shard_map/attend/pallas_call | solution.py:82
  203.9 9.2 %all-to-all-done.1.x_ref = bf16[16,128,512]{2,1,0:T(8,128)(2,1)S(1)} async-done(((bf16[16,128,512]{2,1,0:T(8,128)(2,1)}), bf16[16,128,512]{2,1,0:T(8,128)(2,1)S(1)}, u32[]{:S(2)}, u32[]{:S(2)}) %all-to-all-start.1) | async-done | bytes 2097184 | tf_op jit(solution)/shard_map/all_to_all | solution.py:252
  214.4 4.4 %all-to-all-start.3 = ((bf16[16,128,512]{2,1,0:T(8,128)(2,1)}), bf16[16,128,512]{2,1,0:T(8,128)(2,1)}, u32[]{:S(2)}, u32[]{:S(2)}) async-start(bf16[16,128,512]{2,1,0:T(8,128)(2,1)} %attend.7), calls=%async_computation.3 | async-start | bytes 4194304 | tf_op jit(solution)/shard_map/all_to_all | solution.py:252
  223.1 10.8 %collective-permute-done.1 = bf16[512,512]{1,0:T(8,128)(2,1)} collective-permute-done((bf16[512,512]{1,0:T(8,128)(2,1)S(1)}, bf16[512,512]{1,0:T(8,128)(2,1)}, u32[]{:S(2)}, u32[]{:S(2)}) %collective-permute-start.1) | collective-permute-done | bytes 524320 | tf_op jit(solution)/shard_map/ppermute | solution.py:188
  234.9 9.1 %collective-permute-done.2 = bf16[512,512]{1,0:T(8,128)(2,1)} collective-permute-done((bf16[512,512]{1,0:T(8,128)(2,1)S(1)}, bf16[512,512]{1,0:T(8,128)(2,1)}, u32[]{:S(2)}, u32[]{:S(2)}) %collective-permute-start.2) | collective-permute-done | bytes 524320 | tf_op jit(solution)/shard_map/ppermute | solution.py:188
  246.4 13.5 %attend.5 = bf16[16,128,512]{2,1,0:T(8,128)(2,1)} custom-call(s32[16]{0:T(128)} %reduce_sum.40.block_ref, s32[16]{0:T(128)} %select_reduce_fusion.count_ref, bf16[2048,512]{1,0:T(8,128)(2,1)} %copy-done.5, bf16[2944,256]{1,0:T(8,128)(2,1)} %pad_maximum_fusion.kv_ref), custom_call_target="tpu_custom_call" | custom-call | flops 2684354560 | bytes 5701632 | tf_op jit(solution)/shard_map/attend/pallas_call | solution.py:82
  259.9 6.7 %all-to-all-done.3.x_ref = bf16[16,128,512]{2,1,0:T(8,128)(2,1)} async-done(((bf16[16,128,512]{2,1,0:T(8,128)(2,1)}), bf16[16,128,512]{2,1,0:T(8,128)(2,1)}, u32[]{:S(2)}, u32[]{:S(2)}) %all-to-all-start.3) | async-done | bytes 2097184 | tf_op jit(solution)/shard_map/all_to_all | solution.py:252
  266.6 3.6 %all-to-all-start = ((bf16[16,128,512]{2,1,0:T(8,128)(2,1)}), bf16[16,128,512]{2,1,0:T(8,128)(2,1)S(1)}, u32[]{:S(2)}, u32[]{:S(2)}) async-start(bf16[16,128,512]{2,1,0:T(8,128)(2,1)} %attend.5), calls=%async_computation | async-start | bytes 4194304 | tf_op jit(solution)/shard_map/all_to_all | solution.py:252
  275.4 3.0 place.7.rest_0_
  278.5 3.0 place.8.rest_0_
  281.5 37.1 %all-to-all-done.x_ref = bf16[16,128,512]{2,1,0:T(8,128)(2,1)S(1)} async-done(((bf16[16,128,512]{2,1,0:T(8,128)(2,1)}), bf16[16,128,512]{2,1,0:T(8,128)(2,1)S(1)}, u32[]{:S(2)}, u32[]{:S(2)}) %all-to-all-start) | async-done | bytes 2097184 | tf_op jit(solution)/shard_map/all_to_all | solution.py:252
  320.0 3.0 place.9
  (116 shorter events, 51.0 us)
Async XLA Ops:
  3.9 18.7 %all-to-all-start.2 = ((bf16[4,512,256]{2,1,0:T(8,128)(2,1)}), bf16[4,512,256]{2,1,0:T(8,128)(2,1)S(1)}, u32[]{:S(2)}, u32[]{:S(2)}) async-start(bf16[4,512,256]{2,1,0:T(8,128)(2,1)} %pad_maximum_fusion.2), calls=%async_computation.2 | async-start | bytes 2097152 | tf_op jit(solution)/shard_map/all_to_all | solution.py:170
  22.6 21.4 %all-to-all-start.5 = ((bf16[4,512,256]{2,1,0:T(8,128)(2,1)}), bf16[4,512,256]{2,1,0:T(8,128)(2,1)S(1)}, u32[]{:S(2)}, u32[]{:S(2)}) async-start(bf16[4,512,256]{2,1,0:T(8,128)(2,1)} %pad_maximum_fusion.3), calls=%async_computation.5 | async-start | bytes 2097152 | tf_op jit(solution)/shard_map/all_to_all | solution.py:170
  26.9 14.8 %collective-permute-start.13 = (bf16[896,256]{1,0:T(8,128)(2,1)}, bf16[896,256]{1,0:T(8,128)(2,1)}, u32[]{:S(2)}, u32[]{:S(2)}) collective-permute-start(bf16[896,256]{1,0:T(8,128)(2,1)} %slice.67), channel_id=1, source_target_pairs={{0,4},{4,8},{8,12},{12,16},{16,20},{20,24},{24,28},{1,5},{5,9},{9,... | collective-permute-start | bytes 1376264 | tf_op jit(solution)/shard_map/ppermute | solution.py:141
  55.7 7.2 %copy-start.16 = (bf16[512,128]{1,0:T(8,128)(2,1)S(1)}, bf16[512,128]{1,0:T(8,128)(2,1)}, u32[]{:S(2)}) copy-start(bf16[512,128]{1,0:T(8,128)(2,1)} %get-tuple-element.31) | copy-start | bytes 393220
  55.7 7.2 %copy-start.17 = (bf16[512,128]{1,0:T(8,128)(2,1)S(1)}, bf16[512,128]{1,0:T(8,128)(2,1)}, u32[]{:S(2)}) copy-start(bf16[512,128]{1,0:T(8,128)(2,1)} %get-tuple-element.46) | copy-start | bytes 393220
  55.7 8.1 %copy-start.14 = (bf16[512,128]{1,0:T(8,128)(2,1)S(1)}, bf16[512,128]{1,0:T(8,128)(2,1)}, u32[]{:S(2)}) copy-start(bf16[512,128]{1,0:T(8,128)(2,1)} %get-tuple-element.30) | copy-start | bytes 393220
  55.7 8.1 %copy-start.15 = (bf16[512,128]{1,0:T(8,128)(2,1)S(1)}, bf16[512,128]{1,0:T(8,128)(2,1)}, u32[]{:S(2)}) copy-start(bf16[512,128]{1,0:T(8,128)(2,1)} %get-tuple-element.47) | copy-start | bytes 393220
  55.7 10.6 %copy-start.12 = (bf16[512,128]{1,0:T(8,128)(2,1)S(1)}, bf16[512,128]{1,0:T(8,128)(2,1)}, u32[]{:S(2)}) copy-start(bf16[512,128]{1,0:T(8,128)(2,1)} %get-tuple-element.29) | copy-start | bytes 393220
  55.7 10.6 %copy-start.13 = (bf16[512,128]{1,0:T(8,128)(2,1)S(1)}, bf16[512,128]{1,0:T(8,128)(2,1)}, u32[]{:S(2)}) copy-start(bf16[512,128]{1,0:T(8,128)(2,1)} %get-tuple-element.48) | copy-start | bytes 393220
  55.7 47.7 %all-to-all-start.6 = ((bf16[16,128,256]{2,1,0:T(8,128)(2,1)}), bf16[16,128,256]{2,1,0:T(8,128)(2,1)S(1)}, u32[]{:S(2)}, u32[]{:S(2)}) async-start(bf16[16,128,256]{2,1,0:T(8,128)(2,1)} %attend.9), calls=%async_computation.6 | async-start | bytes 2097152 | tf_op jit(solution)/shard_map/all_to_all | solution.py:252
  63.8 4.7 %collective-permute-start.3 = (bf16[512,512]{1,0:T(8,128)(2,1)}, bf16[512,512]{1,0:T(8,128)(2,1)}, u32[]{:S(2)}, u32[]{:S(2)}) collective-permute-start(bf16[512,512]{1,0:T(8,128)(2,1)} %pad_maximum_fusion.4), channel_id=1, source_target_pairs={{0,1},{1,0},{2,3},{3,2},{4,5},{5,4},{6,7},{7,6},{8,9},{9,8},{10,11... | collective-permute-start | bytes 1572872 | tf_op jit(solution)/shard_map/ppermute | solution.py:188
  64.6 15.1 %collective-permute-start.4 = (bf16[512,512]{1,0:T(8,128)(2,1)}, bf16[512,512]{1,0:T(8,128)(2,1)}, u32[]{:S(2)}, u32[]{:S(2)}) collective-permute-start(bf16[512,512]{1,0:T(8,128)(2,1)} %pad_maximum_fusion.5), channel_id=1, source_target_pairs={{0,2},{1,3},{2,0},{3,1},{4,6},{5,7},{6,4},{7,5},{8,10},{9,11},{10,... | collective-permute-start | bytes 1572872 | tf_op jit(solution)/shard_map/ppermute | solution.py:188
  67.1 22.9 %collective-permute-start.5 = (bf16[512,512]{1,0:T(8,128)(2,1)}, bf16[512,512]{1,0:T(8,128)(2,1)}, u32[]{:S(2)}, u32[]{:S(2)}) collective-permute-start(bf16[512,512]{1,0:T(8,128)(2,1)} %pad_maximum_fusion.6), channel_id=1, source_target_pairs={{0,3},{1,2},{2,1},{3,0},{4,7},{5,6},{6,5},{7,4},{8,11},{9,10},{10,... | collective-permute-start | bytes 1572872 | tf_op jit(solution)/shard_map/ppermute | solution.py:188
  103.4 54.3 %all-to-all-start.4 = ((bf16[16,128,256]{2,1,0:T(8,128)(2,1)}), bf16[16,128,256]{2,1,0:T(8,128)(2,1)}, u32[]{:S(2)}, u32[]{:S(2)}) async-start(bf16[16,128,256]{2,1,0:T(8,128)(2,1)} %attend.8), calls=%async_computation.4 | async-start | bytes 2097152 | tf_op jit(solution)/shard_map/all_to_all | solution.py:252
  115.9 7.2 %collective-permute-start.7 = (bf16[512,512]{1,0:T(8,128)(2,1)}, bf16[512,512]{1,0:T(8,128)(2,1)}, u32[]{:S(2)}, u32[]{:S(2)}) collective-permute-start(bf16[512,512]{1,0:T(8,128)(2,1)} %get-tuple-element.21), channel_id=1, source_target_pairs={{0,1},{1,0},{2,3},{3,2},{4,5},{5,4},{6,7},{7,6},{8,9},{9,8},{10,11... | collective-permute-start | bytes 1572872 | tf_op jit(solution)/shard_map/ppermute | solution.py:188
  115.9 15.1 %collective-permute-start.8 = (bf16[512,512]{1,0:T(8,128)(2,1)}, bf16[512,512]{1,0:T(8,128)(2,1)}, u32[]{:S(2)}, u32[]{:S(2)}) collective-permute-start(bf16[512,512]{1,0:T(8,128)(2,1)} %get-tuple-element.20), channel_id=1, source_target_pairs={{0,2},{1,3},{2,0},{3,1},{4,6},{5,7},{6,4},{7,5},{8,10},{9,11},{10,... | collective-permute-start | bytes 1572872 | tf_op jit(solution)/shard_map/ppermute | solution.py:188
  117.6 23.8 %collective-permute-start.9 = (bf16[512,512]{1,0:T(8,128)(2,1)}, bf16[512,512]{1,0:T(8,128)(2,1)}, u32[]{:S(2)}, u32[]{:S(2)}) collective-permute-start(bf16[512,512]{1,0:T(8,128)(2,1)} %get-tuple-element.19), channel_id=1, source_target_pairs={{0,3},{1,2},{2,1},{3,0},{4,7},{5,6},{6,5},{7,4},{8,11},{9,10},{10,... | collective-permute-start | bytes 1572872 | tf_op jit(solution)/shard_map/ppermute | solution.py:188
  117.8 24.6 %collective-permute-start.6 = (bf16[896,256]{1,0:T(8,128)(2,1)S(1)}, bf16[896,256]{1,0:T(8,128)(2,1)S(1)}, u32[]{:S(2)}, u32[]{:S(2)}) collective-permute-start(bf16[896,256]{1,0:T(8,128)(2,1)S(1)} %slice.65), channel_id=1, source_target_pairs={{0,4},{4,8},{8,12},{12,16},{16,20},{20,24},{24,28},{1,5},{5,9},{9,... | collective-permute-start | bytes 1376264 | tf_op jit(solution)/shard_map/ppermute | solution.py:141
  121.9 20.5 %copy-start.3 = (bf16[2048,256]{1,0:T(8,128)(2,1)S(1)}, bf16[2048,256]{1,0:T(8,128)(2,1)}, u32[]{:S(2)}) copy-start(bf16[2048,256]{1,0:T(8,128)(2,1)} %get-tuple-element.26) | copy-start | bytes 3145732
  157.7 6.9 %copy-start.11 = (bf16[512,512]{1,0:T(8,128)(2,1)S(1)}, bf16[512,512]{1,0:T(8,128)(2,1)}, u32[]{:S(2)}) copy-start(bf16[512,512]{1,0:T(8,128)(2,1)} %get-tuple-element.16) | copy-start | bytes 1572868
  157.7 8.6 %copy-start.10 = (bf16[512,512]{1,0:T(8,128)(2,1)S(1)}, bf16[512,512]{1,0:T(8,128)(2,1)}, u32[]{:S(2)}) copy-start(bf16[512,512]{1,0:T(8,128)(2,1)} %get-tuple-element.15) | copy-start | bytes 1572868
  157.7 55.4 %all-to-all-start.1 = ((bf16[16,128,512]{2,1,0:T(8,128)(2,1)}), bf16[16,128,512]{2,1,0:T(8,128)(2,1)S(1)}, u32[]{:S(2)}, u32[]{:S(2)}) async-start(bf16[16,128,512]{2,1,0:T(8,128)(2,1)} %attend.6), calls=%async_computation.1 | async-start | bytes 4194304 | tf_op jit(solution)/shard_map/all_to_all | solution.py:252
  164.6 2.1 collective-permute-start.10
  164.6 14.9 %collective-permute-start.11 = (bf16[512,512]{1,0:T(8,128)(2,1)S(1)}, bf16[512,512]{1,0:T(8,128)(2,1)S(1)}, u32[]{:S(2)}, u32[]{:S(2)}) collective-permute-start(bf16[512,512]{1,0:T(8,128)(2,1)S(1)} %copy-done.11), channel_id=1, source_target_pairs={{0,2},{1,3},{2,0},{3,1},{4,6},{5,7},{6,4},{7,5},{8,10},{9,11},{10,... | collective-permute-start | bytes 1572872 | tf_op jit(solution)/shard_map/ppermute | solution.py:188
  166.3 23.3 %collective-permute-start.12 = (bf16[512,512]{1,0:T(8,128)(2,1)S(1)}, bf16[512,512]{1,0:T(8,128)(2,1)S(1)}, u32[]{:S(2)}, u32[]{:S(2)}) collective-permute-start(bf16[512,512]{1,0:T(8,128)(2,1)S(1)} %copy-done.10), channel_id=1, source_target_pairs={{0,3},{1,2},{2,1},{3,0},{4,7},{5,6},{6,5},{7,4},{8,11},{9,10},{10,... | collective-permute-start | bytes 1572872 | tf_op jit(solution)/shard_map/ppermute | solution.py:188
  203.9 15.0 %copy-start.9 = (bf16[512,512]{1,0:T(8,128)(2,1)S(1)}, bf16[512,512]{1,0:T(8,128)(2,1)}, u32[]{:S(2)}) copy-start(bf16[512,512]{1,0:T(8,128)(2,1)} %get-tuple-element.23) | copy-start | bytes 1572868
  203.9 16.7 %copy-start.8 = (bf16[512,512]{1,0:T(8,128)(2,1)S(1)}, bf16[512,512]{1,0:T(8,128)(2,1)}, u32[]{:S(2)}) copy-start(bf16[512,512]{1,0:T(8,128)(2,1)} %get-tuple-element.22) | copy-start | bytes 1572868
  214.4 52.2 %all-to-all-start.3 = ((bf16[16,128,512]{2,1,0:T(8,128)(2,1)}), bf16[16,128,512]{2,1,0:T(8,128)(2,1)}, u32[]{:S(2)}, u32[]{:S(2)}) async-start(bf16[16,128,512]{2,1,0:T(8,128)(2,1)} %attend.7), calls=%async_computation.3 | async-start | bytes 4194304 | tf_op jit(solution)/shard_map/all_to_all | solution.py:252
  218.8 3.2 collective-permute-start
  218.9 15.0 %collective-permute-start.1 = (bf16[512,512]{1,0:T(8,128)(2,1)S(1)}, bf16[512,512]{1,0:T(8,128)(2,1)}, u32[]{:S(2)}, u32[]{:S(2)}) collective-permute-start(bf16[512,512]{1,0:T(8,128)(2,1)S(1)} %copy-done.9), channel_id=1, source_target_pairs={{0,2},{1,3},{2,0},{3,1},{4,6},{5,7},{6,4},{7,5},{8,10},{9,11},{10,... | collective-permute-start | bytes 1572872 | tf_op jit(solution)/shard_map/ppermute | solution.py:188
  220.6 23.4 %collective-permute-start.2 = (bf16[512,512]{1,0:T(8,128)(2,1)S(1)}, bf16[512,512]{1,0:T(8,128)(2,1)}, u32[]{:S(2)}, u32[]{:S(2)}) collective-permute-start(bf16[512,512]{1,0:T(8,128)(2,1)S(1)} %copy-done.8), channel_id=1, source_target_pairs={{0,3},{1,2},{2,1},{3,0},{4,7},{5,6},{6,5},{7,4},{8,11},{9,10},{10,... | collective-permute-start | bytes 1572872 | tf_op jit(solution)/shard_map/ppermute | solution.py:188
  266.6 52.0 %all-to-all-start = ((bf16[16,128,512]{2,1,0:T(8,128)(2,1)}), bf16[16,128,512]{2,1,0:T(8,128)(2,1)S(1)}, u32[]{:S(2)}, u32[]{:S(2)}) async-start(bf16[16,128,512]{2,1,0:T(8,128)(2,1)} %attend.5), calls=%async_computation | async-start | bytes 4194304 | tf_op jit(solution)/shard_map/all_to_all | solution.py:252
  (9 other events, 16.9 us)
